TPU v7x, 256 devices: a whole 4x4x8 slice. The times are simulated.
256 devices in a mesh: ctx: 64 (over z_hi, x, y, core), ch: 4 (over z_lo).
Axes of the slice: x: 4, y: 4, z: 8 (z_hi: 2, z_lo: 4; z = z_hi * 4 + z_lo), core: 2. Of those that a mesh axis runs over, the one named last changes fastest.
Arguments:
- tokens: float32 [8192, 3072], P('ctx', 'ch'), may hold values from -6 to 6
- gate_input: float32 [8192, 3072], P('ctx', 'ch'), may hold values from -6 to 6
- cotangent: float32 [8192, 3072], P('ctx', 'ch'), may hold values from -6 to 6
- conv_weight: float32 [2, 4, 3072], P(None, None, 'ch'), may hold values from -3 to 3
- conv_bias: float32 [2, 3072], P(None, 'ch'), may hold values from -3 to 3
- select_weight: float32 [2, 3072, 128], P(None, 'ch'), may hold values from -0.109375 to 0.109375
- step_weight: float32 [2, 96, 3072], P(None, None, 'ch'), may hold values from -0.625 to 0.625
- step_bias: float32 [2, 3072], P(None, 'ch'), may hold values from -6 to -2.5
- decay_log: float32 [2, 16, 3072], P(None, None, 'ch'), may hold values from -12 to 2.75
- skip_gain: float32 [2, 3072], P(None, 'ch'), may hold values from 0.5 to 1.5
Outputs:
- block_out: float32 [8192, 3072], P('ctx', 'ch')
- tokens_grad: float32 [8192, 3072], P('ctx', 'ch')
- gate_grad: float32 [8192, 3072], P('ctx', 'ch')
- select_grad: float32 [2, 3072, 128], P(None, 'ch')
- step_grad: float32 [2, 96, 3072], P(None, None, 'ch')
All inputs are finite; a program needn't handle non-finite values.
Results may differ from a plain program's by a relative error of at most 0.0003.
Values sent between devices are 32-bit elements; how exact they have to be, the bound alone decides.
A program may use at most 64 MiB of HBM per device.

v0:
```python
import jax
import jax.numpy as jnp
from jax import lax
from jax.experimental import pallas as pl
from jax.experimental.pallas import tpu as pltpu
from jax.sharding import PartitionSpec as P

F32 = jnp.float32
HIGH = lax.Precision.HIGHEST
MESH = pl.DeviceIdType.MESH

T = 128
C = 8
L = 16
E = 768
N = 16
R = 96
W = 128
B = E // W
TILES = 64

VM = pl.BlockSpec(memory_space=pltpu.VMEM)


def sds(*shape):
    return jax.ShapeDtypeStruct(shape, F32)


def sigmoid(v):
    return 1.0 / (1.0 + jnp.exp(-v))


def softplus(v):
    return jnp.maximum(v, 0.0) + jnp.log1p(jnp.exp(-jnp.abs(v)))


def rows8(i):
    return pl.ds(pl.multiple_of(i * 8, 8), 8)


def nn(a, b):
    return lax.dot_general(a, b, (((1,), (0,)), ((), ())), precision=HIGH, preferred_element_type=F32)


def nt(a, b):
    return lax.dot_general(a, b, (((1,), (1,)), ((), ())), precision=HIGH, preferred_element_type=F32)


def tn(a, b):
    return lax.dot_general(a, b, (((0,), (0,)), ((), ())), precision=HIGH, preferred_element_type=F32)


class Links:
    def __init__(self, send, recv):
        self.send, self.recv, self.used = send, recv, 0
        self.all = []

    def start(self, src, dst, device):
        k = self.used
        self.used += 1
        copy = pltpu.make_async_remote_copy(
            src_ref=src,
            dst_ref=dst,
            send_sem=self.send.at[k],
            recv_sem=self.recv.at[k],
            device_id=device,
            device_id_type=MESH,
        )
        copy.start()
        self.all.append(copy)
        return copy

    def finish(self):
        for copy in self.all:
            copy.wait_send()


def arrived(copies):
    for copy in copies:
        copy.wait_recv()


def greet(devices):
    barrier = pltpu.get_barrier_semaphore()
    for device in devices:
        pl.semaphore_signal(barrier, inc=1, device_id=device, device_id_type=MESH)
    pl.semaphore_wait(barrier, len(devices))


def plus(a, p, n):
    return lax.rem(a + p, n)


def fill_edges(ext, prev, nxt, has_prev, has_next):
    sub = lax.broadcasted_iota(jnp.int32, (C, E), 0)
    for k in range(3):
        last = ext[3 + L - 3 + k]
        row = jnp.broadcast_to(prev[k : k + 1], (C, E))
        row = jnp.where(has_prev, row, 0.0)
        ext[k] = jnp.where(sub == 0, row, pltpu.roll(last, 1, 0))
        first = ext[3 + k]
        row = jnp.broadcast_to(nxt[k : k + 1], (C, E))
        row = jnp.where(has_next, row, 0.0)
        ext[3 + L + k] = jnp.where(sub == C - 1, row, pltpu.roll(first, C - 1, 0))


def sum_over_ch(links, part, landed, own, total, me, ctx):
    sends = []
    for p in range(1, 4):
        peer = plus(me, p, 4)
        sends.append(links.start(part.at[pl.ds(pl.multiple_of(peer * 64, 64), 64)], landed.at[p - 1], (ctx, peer)))

    def middle():
        arrived(sends)
        mine = pl.ds(pl.multiple_of(me * 64, 64), 64)
        value = part[mine] + landed[0] + landed[1] + landed[2]
        own[...] = value
        total[mine] = value
        return [links.start(own, total.at[mine], (ctx, plus(me, p, 4))) for p in range(1, 4)]

    return middle


def by_lanes(src, dst):
    for b in range(B):
        dst[b] = src[:, b * W : (b + 1) * W]


def every(i):
    return pl.ds(i, C, stride=L)


def front_kernel(tok, cw, cb, sw, act_o, sg_o, proj_o, ext, tiles, prev, nxt, part, landed, own, total, send, recv):
    ctx, me = lax.axis_index("ctx"), lax.axis_index("ch")
    after, before = plus(ctx, 1, TILES), plus(ctx, TILES - 1, TILES)
    greet([(after, me), (before, me)] + [(ctx, plus(me, p, 4)) for p in range(1, 4)])
    links = Links(send, recv)
    halo = [
        links.start(tok.at[pl.ds(T - 8, 8)], prev, (after, me)),
        links.start(tok.at[pl.ds(0, 8)], nxt, (before, me)),
    ]
    by_lanes(tok, tiles)
    for i in range(L):
        for b in range(B):
            ext[3 + i, :, b * W : (b + 1) * W] = tiles[b, every(i)]
    arrived(halo)
    fill_edges(ext, prev[5:8], nxt[0:3], ctx > 0, ctx < TILES - 1)

    def conv(i, carry):
        for d in range(2):
            v = jnp.broadcast_to(cb[d : d + 1], (C, E))
            for k in range(4):
                v = v + cw[d, k : k + 1] * ext[i + (k if d == 0 else 6 - k)]
            s = sigmoid(v)
            act_o[d, rows8(i)] = v * s
            sg_o[d, rows8(i)] = s * (1.0 + v * (1.0 - s))
        return carry

    lax.fori_loop(0, L, conv, 0)
    for d in range(2):
        part[d * T : (d + 1) * T] = nn(act_o[d], sw[d])
    gathers = sum_over_ch(links, part, landed, own, total, me, ctx)()
    arrived(gathers)
    for d in range(2):
        proj_o[d] = total[d * T : (d + 1) * T]
    links.finish()


def front(tok, cw, cb, sw):
    return pl.pallas_call(
        front_kernel,
        out_shape=(sds(2, T, E), sds(2, T, E), sds(2, T, W)),
        in_specs=[VM] * 4,
        out_specs=(VM,) * 3,
        scratch_shapes=[
            pltpu.VMEM((L + 6, C, E), F32),
            pltpu.VMEM((B, T, W), F32),
            pltpu.VMEM((8, E), F32),
            pltpu.VMEM((8, E), F32),
            pltpu.VMEM((2 * T, W), F32),
            pltpu.VMEM((3, 64, W), F32),
            pltpu.VMEM((64, W), F32),
            pltpu.VMEM((2 * T, W), F32),
            pltpu.SemaphoreType.DMA((8,)),
            pltpu.SemaphoreType.DMA((8,)),
        ],
        compiler_params=pltpu.CompilerParams(collective_id=0, has_side_effects=True, vmem_limit_bytes=32 << 20),
        name="front",
    )(tok, cw, cb, sw)


def spread_bases(proj, inb, outb):
    def one(i, carry):
        for d in range(2):
            block = proj[d, rows8(i)]
            for n in range(N):
                inb[d, i, n] = jnp.broadcast_to(block[:, R + n : R + n + 1], (C, W))
                outb[d, i, n] = jnp.broadcast_to(block[:, R + N + n : R + N + n + 1], (C, W))
        return carry

    lax.fori_loop(0, L, one, 0)


def gated(gate, cot, g, i):
    for b in range(B):
        v = gate[b, every(i)]
        g[rows8(i), b * W : (b + 1) * W] = cot[b, every(i)] * v * sigmoid(v)


def local_kernel(
    proj, act, gate, cot, stw, stb, dl, pre_o, step_o, g_o, cu, cd, cp, msg, inb, outb, drv, gates, cots
):
    by_lanes(gate, gates)
    by_lanes(cot, cots)
    for d in range(2):
        pre_o[d] = nn(proj[d][:, :R], stw[d]) + stb[d : d + 1]

    def prepare(i, carry):
        gated(gates, cots, g_o, i)
        for d in range(2):
            st = softplus(pre_o[d, rows8(i)])
            step_o[d, rows8(i)] = st
            drv[d, rows8(i)] = st * act[d, rows8(i)]
        return carry

    lax.fori_loop(0, L, prepare, 0)
    spread_bases(proj, inb, outb)
    H = 8
    for d in range(2):
        for half in range(N // H):

            def block(c, carry, d=d, half=half):
                lanes = pl.ds(pl.multiple_of(c * W, W), W)
                rate = [
                    jnp.broadcast_to(-jnp.exp(dl[d, half * H + j : half * H + j + 1, lanes]), (C, W)) for j in range(H)
                ]

                def advance(i, state):
                    f, p, a = state
                    ii = i if d == 0 else L - 1 - i
                    st, dr = step_o[d, rows8(ii), lanes], drv[d, rows8(ii), lanes]
                    gg = g_o[rows8(ii), lanes]
                    nf, np_, na = [], [], []
                    for j in range(H):
                        dec = jnp.exp(st * rate[j])
                        nf.append(dec * f[j] + inb[d, ii, half * H + j] * dr)
                        q = p[j] * dec
                        np_.append(q)
                        na.append(a[j] + q * (outb[d, ii, half * H + j] * gg))
                    return nf, np_, na

                zero = [jnp.zeros((C, W), F32)] * H
                f, p, a = lax.fori_loop(0, L, advance, (zero, [jnp.ones((C, W), F32)] * H, zero))
                up, down = (cu, cd) if d == 0 else (cd, cu)
                for j in range(H):
                    n = half * H + j
                    row = rows8(d * 12 + (n % 2) * B + c)
                    up[n // 2, row] = f[j]
                    cp[n // 2, row] = p[j]
                    down[n // 2, row] = a[j]
                return carry

            lax.fori_loop(0, B, block, 0)

    def totals(q, carry):
        for k in range(3):
            u = dn = jnp.zeros((C, W), F32)
            pt = jnp.ones((C, W), F32)
            for s in range(C):
                at = pl.ds(k * 64 + s, C, stride=C)
                p = cp[q, at]
                u = p * u + cu[q, at]
                pt = pt * p
                back = pl.ds(k * 64 + C - 1 - s, C, stride=C)
                dn = cp[q, back] * dn + cd[q, back]
            msg[q, k * 8 : k * 8 + 8] = u
            msg[q, 24 + k * 8 : 32 + k * 8] = dn
            msg[q, 48 + k * 8 : 56 + k * 8] = pt
        return carry

    lax.fori_loop(0, 8, totals, 0)


def local(proj, act, gate, cot, stw, stb, dl):
    return pl.pallas_call(
        local_kernel,
        out_shape=(
            sds(2, T, E),
            sds(2, T, E),
            sds(T, E),
            sds(8, 192, W),
            sds(8, 192, W),
            sds(8, 192, W),
            sds(8, 72, W),
        ),
        in_specs=[VM] * 7,
        out_specs=(VM,) * 7,
        scratch_shapes=[
            pltpu.VMEM((2, L, N, C, W), F32),
            pltpu.VMEM((2, L, N, C, W), F32),
            pltpu.VMEM((2, T, E), F32),
            pltpu.VMEM((B, T, W), F32),
            pltpu.VMEM((B, T, W), F32),
        ],
        compiler_params=pltpu.CompilerParams(vmem_limit_bytes=32 << 20),
        name="local",
    )(proj, act, gate, cot, stw, stb, dl)


def carry_kernel(msg, car_o, r1, tot, r2, zs, zr, out, rc, send, recv):
    ctx, ch = lax.axis_index("ctx"), lax.axis_index("ch")
    q, x, z = lax.rem(ctx, 8), lax.rem(ctx // 8, 4), ctx // 32
    base = ctx - q
    xbase = z * 32 + q
    partner = lax.rem(ctx + 32, TILES)
    near = [plus(q, p, 8) for p in range(1, 8)]
    across = [plus(x, p, 4) for p in range(1, 4)]
    greet([(base + k, ch) for k in near] + [(xbase + k * 8, ch) for k in across] + [(partner, ch)])
    links = Links(send, recv)
    copies = [links.start(msg.at[k], r1.at[q], (base + k, ch)) for k in near]
    r1[q] = msg[q]
    arrived(copies)

    def fold(buf, count, u, dn):
        pt = None
        for s in range(count):
            u = buf[s, 48:72] * u + buf[s, 0:24]
            b = count - 1 - s
            dn = buf[b, 48:72] * dn + buf[b, 24:48]
            pt = buf[s, 48:72] if pt is None else pt * buf[s, 48:72]
        return u, dn, pt

    zero = jnp.zeros((24, W), F32)
    u, dn, pt = fold(r1, 8, zero, zero)
    tot[0:24], tot[24:48], tot[48:72] = u, dn, pt
    copies = [links.start(tot, r2.at[x], (xbase + k * 8, ch)) for k in across]
    r2[x] = tot[...]
    arrived(copies)
    u, dn, pt = fold(r2, 4, zero, zero)
    zs[...] = jnp.where(z == 0, u, dn)
    copies = [links.start(zs, zr, (partner, ch))]
    arrived(copies)
    got = zr[...]
    u, dn = jnp.where(z == 1, got, 0.0), jnp.where(z == 0, got, 0.0)
    for s in range(4):
        u = jnp.where(s < x, r2[s, 48:72] * u + r2[s, 0:24], u)
        b = 3 - s
        dn = jnp.where(b > x, r2[b, 48:72] * dn + r2[b, 24:48], dn)
    for s in range(8):
        out[s, 0:24] = u
        u = r1[s, 48:72] * u + r1[s, 0:24]
        b = 7 - s
        out[b, 24:48] = dn
        dn = r1[b, 48:72] * dn + r1[b, 24:48]
    copies = [links.start(out.at[k], rc.at[q], (base + k, ch)) for k in near]
    rc[q] = out[q]
    arrived(copies)
    car_o[...] = rc[...]
    links.finish()


def carries(msg):
    return pl.pallas_call(
        carry_kernel,
        out_shape=sds(8, 48, W),
        in_specs=[VM],
        out_specs=VM,
        scratch_shapes=[
            pltpu.VMEM((8, 72, W), F32),
            pltpu.VMEM((72, W), F32),
            pltpu.VMEM((4, 72, W), F32),
            pltpu.VMEM((24, W), F32),
            pltpu.VMEM((24, W), F32),
            pltpu.VMEM((8, 48, W), F32),
            pltpu.VMEM((8, 48, W), F32),
            pltpu.SemaphoreType.DMA((18,)),
            pltpu.SemaphoreType.DMA((18,)),
        ],
        compiler_params=pltpu.CompilerParams(collective_id=1, has_side_effects=True, vmem_limit_bytes=16 << 20),
        name="carries",
    )(msg)


def sweep_kernel(
    proj, act, gate, cot, stw, dl, skip, pre, step, g, cu, cd, cp, car,
    out_o, gg_o, ga_o, pg_o, sp_o,
    inb, outb, drv, rt, su, sd, ss, go, gi, ya, dg, stt, wpad, gates, cots,
):
    by_lanes(gate, gates)
    by_lanes(cot, cots)
    def starts(q, carry):
        for k in range(3):
            u, dn = car[q, k * 8 : k * 8 + 8], car[q, 24 + k * 8 : 32 + k * 8]
            for s in range(C):
                at = pl.ds(k * 64 + s, C, stride=C)
                su[q, at] = u
                u = cp[q, at] * u + cu[q, at]
                back = pl.ds(k * 64 + C - 1 - s, C, stride=C)
                sd[q, back] = dn
                dn = cp[q, back] * dn + cd[q, back]
        return carry

    lax.fori_loop(0, 8, starts, 0)
    spread_bases(proj, inb, outb)
    for d in range(2):
        for n in range(N):
            rt[d, n] = jnp.broadcast_to(-jnp.exp(dl[d, n : n + 1]), (C, E))

    def prepare(i, carry):
        y = jnp.zeros((C, E), F32)
        for d in range(2):
            a = act[d, rows8(i)]
            drv[d, rows8(i)] = step[d, rows8(i)] * a
            y = y + skip[d : d + 1] * a
        ya[rows8(i)] = y
        return carry

    lax.fori_loop(0, L, prepare, 0)
    H, Q = 8, 3
    QW = Q * W

    def folded(v):
        r = v[:, :W]
        for k in range(1, Q):
            r = r + v[:, k * W : (k + 1) * W]
        return r

    def wide(v):
        return jnp.concatenate([v] * Q, axis=1)

    for d in range(2):
        fs, as_ = (su, sd) if d == 0 else (sd, su)
        for half in range(N // H):
            for cb in range(B // Q):
                lanes = pl.ds(cb * QW, QW)

                def begin(src, j, d=d, half=half, cb=cb):
                    n = half * H + j
                    row = d * 12 + (n % 2) * B + cb * Q
                    return jnp.concatenate([src[n // 2, pl.ds((row + k) * 8, 8)] for k in range(Q)], axis=1)

                def forward(i, state, d=d, half=half, cb=cb, lanes=lanes):
                    ii = i if d == 0 else L - 1 - i
                    st, dr = step[d, rows8(ii), lanes], drv[d, rows8(ii), lanes]
                    gg = g[rows8(ii), lanes]
                    y = ya[rows8(ii), lanes]
                    new = []
                    for j in range(H):
                        n = half * H + j
                        s = jnp.exp(st * rt[d, n, :, lanes]) * state[j] + wide(inb[d, ii, n]) * dr
                        y = y + wide(outb[d, ii, n]) * s
                        v = folded(s * gg)
                        go[d, ii, n] = v if cb == 0 else go[d, ii, n] + v
                        ss[i + 1, j] = s
                        new.append(s)
                    ya[rows8(ii), lanes] = y
                    return new

                first = [begin(fs, j) for j in range(H)]
                for j in range(H):
                    ss[0, j] = first[j]
                lax.fori_loop(0, L, forward, first)

                def retreat(t, carried, d=d, half=half, cb=cb, lanes=lanes):
                    i = L - 1 - t
                    ii = i if d == 0 else L - 1 - i
                    st, dr = step[d, rows8(ii), lanes], drv[d, rows8(ii), lanes]
                    gg = g[rows8(ii), lanes]
                    if half == 0:
                        a1 = a2 = jnp.zeros((C, QW), F32)
                    else:
                        a1, a2 = stt[d, rows8(ii), lanes], dg[d, rows8(ii), lanes]
                    new = []
                    for j in range(H):
                        n = half * H + j
                        rate = rt[d, n, :, lanes]
                        adj = carried[j] + wide(outb[d, ii, n]) * gg
                        back = jnp.exp(st * rate) * adj
                        a1 = a1 + (back * ss[i, j]) * rate
                        a2 = a2 + adj * wide(inb[d, ii, n])
                        v = folded(adj * dr)
                        gi[d, ii, n] = v if cb == 0 else gi[d, ii, n] + v
                        new.append(back)
                    stt[d, rows8(ii), lanes] = a1
                    dg[d, rows8(ii), lanes] = a2
                    return new

                lax.fori_loop(0, L, retreat, [begin(as_, j) for j in range(H)])

    def close(i, carry):
        at = rows8(i)
        for b in range(B):
            v, ct, y = gates[b, every(i)], cots[b, every(i)], ya[at, b * W : (b + 1) * W]
            s = sigmoid(v)
            gates[b, every(i)] = y * v * s
            cots[b, every(i)] = ct * y * (s * (1.0 + v * (1.0 - s)))
        for d in range(2):
            slope = dg[d, at]
            ga_o[d, at] = g[at] * skip[d : d + 1] + slope * step[d, at]
            stt[d, at] = (stt[d, at] + slope * act[d, at]) * sigmoid(pre[d, at])
        return carry

    lax.fori_loop(0, L, close, 0)
    for b in range(B):
        out_o[:, b * W : (b + 1) * W] = gates[b]
        gg_o[:, b * W : (b + 1) * W] = cots[b]
    wpad[...] = jnp.zeros_like(wpad)
    lane = lax.broadcasted_iota(jnp.int32, (C, W), 1)
    for d in range(2):
        wpad[d, 0:R] = stw[d]
        sp_o[d] = tn(proj[d], stt[d])[:R]
        pg_o[d] = nt(stt[d], wpad[d])

    def bases(i, carry):
        for d in range(2):
            v = pg_o[d, rows8(i)]
            for n in range(N):
                v = v + jnp.where(lane == R + n, jnp.sum(gi[d, i, n], axis=1, keepdims=True), 0.0)
                v = v + jnp.where(lane == R + N + n, jnp.sum(go[d, i, n], axis=1, keepdims=True), 0.0)
            pg_o[d, rows8(i)] = v
        return carry

    lax.fori_loop(0, L, bases, 0)


def sweep(*args):
    return pl.pallas_call(
        sweep_kernel,
        out_shape=(sds(T, E), sds(T, E), sds(2, T, E), sds(2, T, W), sds(2, R, E)),
        in_specs=[VM] * 14,
        out_specs=(VM,) * 5,
        scratch_shapes=[
            pltpu.VMEM((2, L, N, C, W), F32),
            pltpu.VMEM((2, L, N, C, W), F32),
            pltpu.VMEM((2, T, E), F32),
            pltpu.VMEM((2, N, C, E), F32),
            pltpu.VMEM((8, 192, W), F32),
            pltpu.VMEM((8, 192, W), F32),
            pltpu.VMEM((L + 1, 8, C, 3 * W), F32),
            pltpu.VMEM((2, L, N, C, W), F32),
            pltpu.VMEM((2, L, N, C, W), F32),
            pltpu.VMEM((T, E), F32),
            pltpu.VMEM((2, T, E), F32),
            pltpu.VMEM((2, T, E), F32),
            pltpu.VMEM((2, W, E), F32),
            pltpu.VMEM((B, T, W), F32),
            pltpu.VMEM((B, T, W), F32),
        ],
        compiler_params=pltpu.CompilerParams(vmem_limit_bytes=48 << 20),
        name="sweep",
    )(*args)


def back_kernel(
    pg, act, sg, ga, sw, cw, sp,
    tg_o, selg_o, stepg_o,
    landed, own, total, slp, ext0, ext1, send0, send1, prev, nxt, tgp, tiles,
    s_r0, s0, s_r1, s1, s_r2, s2, s_r3, s3, s_x, s_y, s_out,
    t_r0, t0, t_r1, t1, t_r2, t2, t_r3, t3, t_y, t_x, t_out,
    send, recv,
):
    ctx, me = lax.axis_index("ctx"), lax.axis_index("ch")
    after, before = plus(ctx, 1, TILES), plus(ctx, TILES - 1, TILES)
    core, y, x = lax.rem(ctx, 2), lax.rem(ctx // 2, 4), lax.rem(ctx // 8, 4)
    other = 1 - core
    mate = (ctx - core + other, me)
    far = (lax.rem(ctx + 32, TILES), me)
    ys = [plus(y, p, 4) for p in range(1, 4)]
    xs = [plus(x, p, 4) for p in range(1, 4)]
    ydev = [(ctx + (k - y) * 2, me) for k in ys]
    xdev = [(ctx + (k - x) * 8, me) for k in xs]
    greet([(after, me), (before, me), mate, far] + ydev + xdev + [(ctx, plus(me, p, 4)) for p in range(1, 4)])
    links = Links(send, recv)

    def rows(k, n):
        return pl.ds(pl.multiple_of(k * n, 8), n)

    def scatter(src, n, ks, devices, dst):
        return [links.start(src.at[rows(k, n)], dst.at[p], dev) for p, (k, dev) in enumerate(zip(ks, devices))]

    def summed(src, k, n, dst):
        return src[rows(k, n)] + dst[0] + dst[1] + dst[2]

    step_core = [links.start(sp.at[other], s_r0, mate)]
    middle = sum_over_ch(links, pg, landed, own, total, me, ctx)
    arrived(step_core)
    s0[...] = sp[core] + s_r0[...]
    step_y = scatter(s0, 24, ys, ydev, s_r1)
    gathers = middle()
    arrived(step_y)
    s1[0:24] = summed(s0, y, 24, s_r1)
    s1[24:32] = jnp.zeros((8, E), F32)
    step_x = scatter(s1, 8, xs, xdev, s_r2)
    arrived(gathers)
    for d in range(2):
        slp[d] = tn(act[d], total[d * T : (d + 1) * T])
    sel_core = [links.start(slp.at[other], t_r0, mate)]
    for d, ext in enumerate((ext0, ext1)):
        tgp[...] = nt(total[d * T : (d + 1) * T], sw[d])

        def conv_grad(i, carry, d=d, ext=ext):
            ext[3 + i] = (ga[d, rows8(i)] + tgp[rows8(i)]) * sg[d, rows8(i)]
            return carry

        lax.fori_loop(0, L, conv_grad, 0)
    for k in range(3):
        send0[k : k + 1] = ext0[3 + k, 0:1]
        send1[k : k + 1] = ext1[3 + L - 3 + k, C - 1 : C]
    halo = [links.start(send0, nxt, (before, me)), links.start(send1, prev, (after, me))]
    arrived(sel_core)
    t0[...] = slp[core] + t_r0[...]
    sel_x = scatter(t0, 192, xs, xdev, t_r1)
    arrived(step_x)
    s2[...] = summed(s1, x, 8, s_r2)
    step_z = [links.start(s2, s_r3, far)]
    arrived(halo)
    fill_edges(ext0, prev[0:3], nxt[0:3], ctx > 0, ctx < TILES - 1)
    fill_edges(ext1, prev[0:3], nxt[0:3], ctx > 0, ctx < TILES - 1)

    def conv_back(i, carry):
        v = jnp.zeros((C, E), F32)
        for k in range(4):
            v = v + cw[0, k : k + 1] * ext0[i + 6 - k] + cw[1, k : k + 1] * ext1[i + k]
        for b in range(B):
            tiles[b, every(i)] = v[:, b * W : (b + 1) * W]
        return carry

    lax.fori_loop(0, L, conv_back, 0)
    for b in range(B):
        tg_o[:, b * W : (b + 1) * W] = tiles[b]
    arrived(sel_x)
    t1[...] = summed(t0, x, 192, t_r1)
    sel_y = scatter(t1, 48, ys, ydev, t_r2)
    arrived(step_z)
    v = s2[...] + s_r3[...]
    s3[...] = v
    s_x[rows(x, 8)] = v
    step_x = [links.start(s3, s_x.at[rows(x, 8)], dev) for dev in xdev]
    arrived(sel_y)
    t2[...] = summed(t1, y, 48, t_r2)
    sel_z = [links.start(t2, t_r3, far)]
    arrived(step_x)
    s_y[rows(y, 24)] = s_x[0:24]
    step_y = [links.start(s_x.at[pl.ds(0, 24)], s_y.at[rows(y, 24)], dev) for dev in ydev]
    arrived(sel_z)
    v = t2[...] + t_r3[...]
    t3[...] = v
    t_y[rows(y, 48)] = v
    sel_y = [links.start(t3, t_y.at[rows(y, 48)], dev) for dev in ydev]
    arrived(step_y)
    step_core = [links.start(s_y, s_out, mate)]
    arrived(sel_y)
    t_x[rows(x, 192)] = t_y[...]
    sel_x = [links.start(t_y, t_x.at[rows(x, 192)], dev) for dev in xdev]
    stepg_o[core] = s_y[...]
    arrived(step_core)
    stepg_o[other] = s_out[...]
    arrived(sel_x)
    sel_core = [links.start(t_x, t_out, mate)]
    selg_o[core] = t_x[...]
    arrived(sel_core)
    selg_o[other] = t_out[...]
    links.finish()


def back(*args):
    v = lambda *shape: pltpu.VMEM(shape, F32)
    return pl.pallas_call(
        back_kernel,
        out_shape=(sds(T, E), sds(2, E, W), sds(2, R, E)),
        in_specs=[VM] * 7,
        out_specs=(VM,) * 3,
        scratch_shapes=[
            v(3, 64, W), v(64, W), v(2 * T, W), v(2, E, W), v(L + 6, C, E), v(L + 6, C, E),
            v(8, E), v(8, E), v(8, E), v(8, E), v(T, E), v(B, T, W),
            v(R, E), v(R, E), v(3, 24, E), v(32, E), v(3, 8, E), v(8, E), v(8, E), v(8, E), v(32, E), v(R, E), v(R, E),
            v(E, W), v(E, W), v(3, 192, W), v(192, W), v(3, 48, W), v(48, W), v(48, W), v(48, W), v(192, W), v(E, W),
            v(E, W),
            pltpu.SemaphoreType.DMA((38,)),
            pltpu.SemaphoreType.DMA((38,)),
        ],
        compiler_params=pltpu.CompilerParams(collective_id=2, has_side_effects=True, vmem_limit_bytes=40 << 20),
        name="back",
    )(*args)


def on_device(tok, gate, cot, cw, cb, sw, stw, stb, dl, skip):
    act, sg, proj = front(tok, cw, cb, sw)
    pre, step, g, cu, cd, cp, msg = local(proj, act, gate, cot, stw, stb, dl)
    car = carries(msg)
    out, gg, ga, pg, sp = sweep(proj, act, gate, cot, stw, dl, skip, pre, step, g, cu, cd, cp, car)
    tg, selg, stepg = back(pg.reshape(2 * T, W), act, sg, ga, sw, cw, sp)
    return out, tg, gg, selg, stepg


def solution(mesh):
    row = P("ctx", "ch")
    in_specs = (
        row,
        row,
        row,
        P(None, None, "ch"),
        P(None, "ch"),
        P(None, "ch", None),
        P(None, None, "ch"),
        P(None, "ch"),
        P(None, None, "ch"),
        P(None, "ch"),
    )
    out_specs = (row, row, row, P(None, "ch", None), P(None, None, "ch"))
    return jax.shard_map(on_device, mesh=mesh, in_specs=in_specs, out_specs=out_specs, check_vma=False)
```

profile of v0, /device:TPU:1, one launch (start us, length us, event | category | flops | bytes accessed | tf_op | source)
XLA Modules:
  0.0 136.3 jit_solution(5725042697282986685)
XLA Ops:
  0.6 0.0 copy-start
  0.6 1.1 copy-done
  1.8 0.0 copy-start.10
  1.8 1.0 copy-done.10
  2.8 0.0 copy-start.11
  2.8 0.7 copy-done.11
  3.5 0.0 copy-start.13
  3.5 0.7 copy-done.13
  4.2 0.0 copy-start.2
  4.2 0.0 copy-start.3
  4.2 0.0 copy-start.9
  4.2 0.0 copy-start.15
  4.2 22.0 %front.1 = (f32[2,128,768]{2,1,0:T(8,128)S(1)}, f32[2,128,768]{2,1,0:T(8,128)S(1)}, f32[2,128,128]{2,1,0:T(8,128)S(1)}) custom-call(f32[128,768]{1,0:T(8,128)S(1)} %copy-done.10, f32[2,4,768]{2,1,0:T(4,128)S(1)} %copy-done.11, f32[2,768]{1,0:T(2,128)S(1)} %copy-done.13, f32[2,768,128]{2,1,0:T(8,128)S(1)} %copy-done), custom_call_target="tpu_custom_call" | custom-call | tf_op jit(solution)/shard_map/front/pallas_call | solution.py:170
  26.2 0.0 copy-done.2
  26.2 0.0 copy-done.3
  26.3 0.0 copy-done.9
  26.3 0.0 copy-done.15
  26.3 0.0 copy-start.4
  26.3 1.0 copy-done.4
  27.3 14.0 %local.1 = (f32[2,128,768]{2,1,0:T(8,128)S(1)}, f32[2,128,768]{2,1,0:T(8,128)S(1)}, f32[128,768]{1,0:T(8,128)S(1)}, f32[8,192,128]{2,1,0:T(8,128)S(1)}, f32[8,19...) custom-call(f32[2,128,128]{2,1,0:T(8,128)S(1)} %get-tuple-element.23.proj, ...), custom_call_target="tpu_custom_call" | custom-call | tf_op jit(solution)/shard_map/local/pallas_call | solution.py:285
  41.3 0.0 copy-start.6
  41.3 0.9 copy-done.6
  42.2 0.0 copy-start.7
  42.2 0.9 copy-done.7
  43.1 0.0 copy-start.8
  43.1 0.9 copy-done.8
  44.0 0.0 copy-start.5
  44.0 0.0 copy-start.14
  44.0 25.5 %carries.1.car = f32[8,48,128]{2,1,0:T(8,128)S(1)} custom-call(f32[8,72,128]{2,1,0:T(8,128)S(1)} %get-tuple-element.31.msg), custom_call_target="tpu_custom_call" | custom-call | tf_op jit(solution)/shard_map/carries/pallas_call | solution.py:363
  69.4 0.0 copy-done.5
  69.4 0.0 copy-done.14
  69.4 0.0 copy-start.1
  69.5 0.0 copy-start.12
  69.5 22.3 %sweep.1 = (f32[128,768]{1,0:T(8,128)}, f32[128,768]{1,0:T(8,128)}, f32[2,128,768]{2,1,0:T(8,128)S(1)}, f32[2,128,128]{2,1,0:T(8,128)S(1)}, f32[2,96,768]{2,1,0:T(8,128)S(1)}) custom-call(f32[2,128,128]{2,1,0:T(8,128)S(1)} %get-tuple-element.23.proj, f32[2,128,768]{2,1,0:T(8,128)S(1)} %get-tuple-element.24.act, f32[128,768]{1,0:T(8,128)S(1)} %copy-done.3, ...), custom_call_target="tpu_custom_call" | custom-call | tf_op jit(solution)/shard_map/sweep/pallas_call | solution.py:527
  91.8 0.0 copy-done.1
  91.8 0.0 copy-done.12
  91.8 42.0 %back.1 = (f32[128,768]{1,0:T(8,128)S(1)}, f32[2,768,128]{2,1,0:T(8,128)S(1)}, f32[2,96,768]{2,1,0:T(8,128)S(1)}) custom-call(f32[256,128]{1,0:T(8,128)S(1)} %bitcast.1, f32[2,128,768]{2,1,0:T(8,128)S(1)} %get-tuple-element.24.act, f32[2,128,768]{2,1,0:T(8,128)S(1)} %get-tuple-element.34.sg, f32[2,128,768]{2,1,0:T(8,128)S(1)} %get-tuple-element.35.ga, ...), custom_call_target="tpu_custom_call" | custom-call | tf_op jit(solution)/shard_map/back/pallas_call | solution.py:668
  133.8 0.7 copy.18
  134.6 0.9 copy.19
  135.5 0.8 copy.20
Async XLA Ops:
  0.6 1.1 copy-start
  1.8 1.0 copy-start.10
  2.8 0.7 copy-start.11
  3.5 0.7 copy-start.13
  4.2 22.0 %copy-start.2 = (f32[2,96,768]{2,1,0:T(8,128)S(1)}, f32[2,96,768]{2,1,0:T(8,128)}, u32[]{:S(2)}) copy-start(f32[2,96,768]{2,1,0:T(8,128)} %stw.3) | copy-start | bytes 1769476
  4.2 22.0 %copy-start.3 = (f32[128,768]{1,0:T(8,128)S(1)}, f32[128,768]{1,0:T(8,128)}, u32[]{:S(2)}) copy-start(f32[128,768]{1,0:T(8,128)} %gate.3) | copy-start | bytes 1179652
  4.2 22.1 %copy-start.9 = (f32[2,16,768]{2,1,0:T(8,128)S(1)}, f32[2,16,768]{2,1,0:T(8,128)}, u32[]{:S(2)}) copy-start(f32[2,16,768]{2,1,0:T(8,128)} %dl.3) | copy-start | bytes 294916
  4.2 22.1 %copy-start.15 = (f32[2,768]{1,0:T(2,128)S(1)}, f32[2,768]{1,0:T(2,128)}, u32[]{:S(2)}) copy-start(f32[2,768]{1,0:T(2,128)} %stb.1) | copy-start | bytes 18436
  26.3 1.0 copy-start.4
  41.3 0.9 copy-start.6
  42.2 0.9 copy-start.7
  43.1 0.9 copy-start.8
  44.0 25.5 %copy-start.5 = (f32[128,768]{1,0:T(8,128)S(1)}, f32[128,768]{1,0:T(8,128)}, u32[]{:S(2)}) copy-start(f32[128,768]{1,0:T(8,128)} %cot.3) | copy-start | bytes 1179652
  44.0 25.5 %copy-start.14 = (f32[2,768]{1,0:T(2,128)S(1)}, f32[2,768]{1,0:T(2,128)}, u32[]{:S(2)}) copy-start(f32[2,768]{1,0:T(2,128)} %skip.1) | copy-start | bytes 18436
  69.4 22.4 %copy-start.1 = (f32[2,768,128]{2,1,0:T(8,128)S(1)}, f32[2,768,128]{2,1,0:T(8,128)}, u32[]{:S(2)}) copy-start(f32[2,768,128]{2,1,0:T(8,128)} %sw.3) | copy-start | bytes 2359300
  69.5 22.3 %copy-start.12 = (f32[2,4,768]{2,1,0:T(4,128)S(1)}, f32[2,4,768]{2,1,0:T(4,128)}, u32[]{:S(2)}) copy-start(f32[2,4,768]{2,1,0:T(4,128)} %cw.3) | copy-start | bytes 73732
where the time goes:
time: 137 us; the launch traced here: 136 us
  Pallas kernels  126 us (92%)
  local copies, waits for them, and re-layouts  9.68 us (7%)
    pallas_call x1, Pallas kernels, back(): pl.pallas_call(back_kernel, out_shape=(sds(T, E), sds(2, E, W), sds(2, R,...  42 us
    pallas_call x1, Pallas kernels, carries(): pl.pallas_call(carry_kernel, out_shape=sds(8, 48, W), in_specs=[VM], out_...  25.5 us
    pallas_call x1, Pallas kernels, sweep(): pl.pallas_call(sweep_kernel, out_shape=(sds(T, E), sds(T, E), sds(2, T, E...  22.3 us
    pallas_call x1, Pallas kernels, front(): pl.pallas_call(front_kernel, out_shape=(sds(2, T, E), sds(2, T, E), sds(2...  22 us
    pallas_call x1, Pallas kernels, local(): pl.pallas_call(local_kernel, out_shape=(sds(2, T, E), sds(2, T, E), sds(T...  14 us
    unnamed x35, local copies, waits for them, and re-layouts  9.68 us

commit v1 on v0

v1 whole, which is shorter than its diff:
```python
import jax
import jax.numpy as jnp
from jax import lax
from jax.experimental import pallas as pl
from jax.experimental.pallas import tpu as pltpu
from jax.sharding import PartitionSpec as P

F32 = jnp.float32
HIGH = lax.Precision.HIGHEST
MESH = pl.DeviceIdType.MESH

T = 128
C = 8
L = 16
E = 768
N = 16
R = 96
W = 128
B = E // W
TILES = 64

VM = pl.BlockSpec(memory_space=pltpu.VMEM)


def sds(*shape):
    return jax.ShapeDtypeStruct(shape, F32)


LOG2E = 1.4426950408889634
LN2 = 0.6931471805599453


def sigmoid(v):
    return 1.0 / (1.0 + jnp.exp(-v))


def softplus(v):
    return jnp.maximum(v, 0.0) + jnp.log1p(jnp.exp(-jnp.abs(v)))


def rows8(i):
    return pl.ds(pl.multiple_of(i * 8, 8), 8)


def nn(a, b):
    return lax.dot_general(a, b, (((1,), (0,)), ((), ())), precision=HIGH, preferred_element_type=F32)


def nt(a, b):
    return lax.dot_general(a, b, (((1,), (1,)), ((), ())), precision=HIGH, preferred_element_type=F32)


def tn(a, b):
    return lax.dot_general(a, b, (((0,), (0,)), ((), ())), precision=HIGH, preferred_element_type=F32)


class Links:
    def __init__(self, send, recv):
        self.send, self.recv, self.used = send, recv, 0
        self.all = []

    def start(self, src, dst, device):
        k = self.used
        self.used += 1
        copy = pltpu.make_async_remote_copy(
            src_ref=src,
            dst_ref=dst,
            send_sem=self.send.at[k],
            recv_sem=self.recv.at[k],
            device_id=device,
            device_id_type=MESH,
        )
        copy.start()
        self.all.append(copy)
        return copy

    def finish(self):
        for copy in self.all:
            copy.wait_send()


def arrived(copies):
    for copy in copies:
        copy.wait_recv()


def greet(devices):
    barrier = pltpu.get_barrier_semaphore()
    for device in devices:
        pl.semaphore_signal(barrier, inc=1, device_id=device, device_id_type=MESH)
    pl.semaphore_wait(barrier, len(devices))


def plus(a, p, n):
    return lax.rem(a + p, n)


def fill_edges(ext, prev, nxt, has_prev, has_next):
    sub = lax.broadcasted_iota(jnp.int32, (C, E), 0)
    for k in range(3):
        last = ext[3 + L - 3 + k]
        row = jnp.broadcast_to(prev[k : k + 1], (C, E))
        row = jnp.where(has_prev, row, 0.0)
        ext[k] = jnp.where(sub == 0, row, pltpu.roll(last, 1, 0))
        first = ext[3 + k]
        row = jnp.broadcast_to(nxt[k : k + 1], (C, E))
        row = jnp.where(has_next, row, 0.0)
        ext[3 + L + k] = jnp.where(sub == C - 1, row, pltpu.roll(first, C - 1, 0))


def by_lanes(src, dst):
    for b in range(B):
        dst[b] = src[:, b * W : (b + 1) * W]


def every(i):
    return pl.ds(i, C, stride=L)


def rows(k, n):
    return pl.ds(pl.multiple_of(k * n, 8), n)


class ChannelSum:
    def __init__(self, links, part, landed, own, total, me, ctx):
        self.links, self.part, self.landed, self.own, self.total = links, part, landed, own, total
        self.me, self.peers = me, [(ctx, plus(me, p, 4)) for p in range(1, 4)]

    def scatter(self):
        self.copies = [
            self.links.start(self.part.at[rows(peer[1], 32)], self.landed.at[p], peer)
            for p, peer in enumerate(self.peers)
        ]

    def gather(self):
        arrived(self.copies)
        mine = rows(self.me, 32)
        value = self.part[mine] + self.landed[0] + self.landed[1] + self.landed[2]
        self.own[...] = value
        self.total[mine] = value
        self.copies = [self.links.start(self.own, self.total.at[mine], peer) for peer in self.peers]

    def wait(self):
        arrived(self.copies)


class TileSum:
    def __init__(self, links, place, src, r0, t0, r1, t2, r3, t3, t4, fin):
        self.links, self.place, self.src = links, place, src
        self.r0, self.t0, self.r1, self.t2, self.r3, self.t3, self.t4, self.fin = r0, t0, r1, t2, r3, t3, t4, fin

    def core(self):
        self.copies = [self.links.start(self.src.at[rows(1 - self.place.core, 384)], self.r0, self.place.mate)]

    def scatter(self):
        arrived(self.copies)
        self.t0[...] = self.src[rows(self.place.core, 384)] + self.r0[...]
        self.copies = [
            self.links.start(self.t0.at[rows(k, 24)], self.r1.at[p], dev)
            for p, (k, dev) in enumerate(self.place.plane)
        ]

    def far(self):
        arrived(self.copies)
        v = self.t0[rows(self.place.k, 24)]
        for p in range(15):
            v = v + self.r1[p]
        self.t2[...] = v
        self.copies = [self.links.start(self.t2, self.r3, self.place.far)]

    def gather(self):
        arrived(self.copies)
        v = self.t2[...] + self.r3[...]
        mine = rows(self.place.k, 24)
        self.t3[...] = v
        self.t4[mine] = v
        self.copies = [self.links.start(self.t3, self.t4.at[mine], dev) for _, dev in self.place.plane]

    def join(self):
        arrived(self.copies)
        self.copies = [self.links.start(self.t4, self.fin, self.place.mate)]

    def end(self, write):
        write(self.place.core, self.t4)
        arrived(self.copies)
        write(1 - self.place.core, self.fin)


class Place:
    def __init__(self):
        ctx, me = lax.axis_index("ctx"), lax.axis_index("ch")
        self.ctx, self.me = ctx, me
        self.after, self.before = (plus(ctx, 1, TILES), me), (plus(ctx, TILES - 1, TILES), me)
        self.core, self.y, self.x = lax.rem(ctx, 2), lax.rem(ctx // 2, 4), lax.rem(ctx // 8, 4)
        self.q, self.z = lax.rem(ctx, 8), ctx // 32
        self.mate = (ctx - self.core + 1 - self.core, me)
        self.far = (lax.rem(ctx + 32, TILES), me)
        self.k = self.x * 4 + self.y
        self.plane = []
        for dx in range(4):
            for dy in range(4):
                if dx or dy:
                    x, y = plus(self.x, dx, 4), plus(self.y, dy, 4)
                    self.plane.append((x * 4 + y, (ctx + (x - self.x) * 8 + (y - self.y) * 2, me)))
        base = ctx - self.q
        self.near = [(k, (base + k, me)) for k in [plus(self.q, p, 8) for p in range(1, 8)]]
        self.across = [(ctx + (plus(self.x, p, 4) - self.x) * 8, me) for p in range(1, 4)]
        self.ch = [(ctx, plus(me, p, 4)) for p in range(1, 4)]

    def everyone(self):
        plane = [dev for _, dev in self.plane]
        return [self.after, self.before, self.far] + plane + [dev for _, dev in self.near] + self.ch


def exchange_carries(links, place, msg, r1, tot, r2, zs, zr, out, rc):
    q, x, z = place.q, place.x, place.z
    copies = [links.start(msg.at[k], r1.at[q], dev) for k, dev in place.near]
    r1[q] = msg[q]
    arrived(copies)

    def fold(buf, count, u, dn):
        pt = None
        for s in range(count):
            u = buf[s, 48:72] * u + buf[s, 0:24]
            b = count - 1 - s
            dn = buf[b, 48:72] * dn + buf[b, 24:48]
            pt = buf[s, 48:72] if pt is None else pt * buf[s, 48:72]
        return u, dn, pt

    zero = jnp.zeros((24, W), F32)
    u, dn, pt = fold(r1, 8, zero, zero)
    tot[0:24], tot[24:48], tot[48:72] = u, dn, pt
    copies = [links.start(tot, r2.at[x], dev) for dev in place.across]
    r2[x] = tot[...]
    arrived(copies)
    u, dn, pt = fold(r2, 4, zero, zero)
    zs[...] = jnp.where(z == 0, u, dn)
    arrived([links.start(zs, zr, place.far)])
    got = zr[...]
    u, dn = jnp.where(z == 1, got, 0.0), jnp.where(z == 0, got, 0.0)
    for s in range(4):
        u = jnp.where(s < x, r2[s, 48:72] * u + r2[s, 0:24], u)
        b = 3 - s
        dn = jnp.where(b > x, r2[b, 48:72] * dn + r2[b, 24:48], dn)
    for s in range(8):
        out[s, 0:24] = u
        u = r1[s, 48:72] * u + r1[s, 0:24]
        b = 7 - s
        out[b, 24:48] = dn
        dn = r1[b, 48:72] * dn + r1[b, 24:48]
    copies = [links.start(out.at[k], rc.at[q], dev) for k, dev in place.near]
    rc[q] = out[q]
    arrived(copies)


def block_kernel(
    tok_h, gate_h, cot_h, cw_h, cb_h, sw_h, stw_h, stb_h, dl_h, skip_h,
    out_o, tg_o, gg_o, selg_o, stepg_o,
    tok, gate, cot, cw, cb, sw, stw, stb, dl, skip, in_sem,
    tiles, gates, cots, prev, nxt, prev2, nxt2, send0, send1, ext0, ext1,
    act, sg, part, landed, own, proj, part2, landed2, own2, gp,
    pre, step, drv, g, rt, inb, outb, dec, cu, cd, cp, su, sd,
    msg, cr1, ctot, cr2, czs, czr, cout, crc,
    ss, go, gi, ya, dg, stt, wpad, tgp,
    w_src, w_r0, w_t0, w_r1, w_t2, w_r3, w_t3, w_t4, w_fin,
    send, recv,
):
    pairs = (
        (tok_h, tok), (cw_h, cw), (cb_h, cb), (sw_h, sw), (gate_h, gate), (cot_h, cot),
        (stw_h, stw), (stb_h, stb), (dl_h, dl), (skip_h, skip),
    )
    loads = [pltpu.make_async_copy(a, b, in_sem.at[k]) for k, (a, b) in enumerate(pairs)]
    for load in loads:
        load.start()
    place = Place()
    ctx, me = place.ctx, place.me
    greet(place.everyone())
    links = Links(send, recv)
    halo = [
        links.start(tok_h.at[pl.ds(T - 8, 8)], prev, place.after),
        links.start(tok_h.at[pl.ds(0, 8)], nxt, place.before),
    ]
    loads[0].wait()
    by_lanes(tok, tiles)
    for i in range(L):
        for b in range(B):
            ext0[3 + i, :, b * W : (b + 1) * W] = tiles[b, every(i)]
    for load in loads[1:4]:
        load.wait()
    arrived(halo)
    fill_edges(ext0, prev[5:8], nxt[0:3], ctx > 0, ctx < TILES - 1)
    sums = [ChannelSum(links, part.at[d], landed.at[d], own.at[d], proj.at[d], me, ctx) for d in range(2)]
    for d in range(2):

        def conv(i, carry, d=d):
            v = jnp.broadcast_to(cb[d : d + 1], (C, E))
            for k in range(4):
                v = v + cw[d, k : k + 1] * ext0[i + (k if d == 0 else 6 - k)]
            s = sigmoid(v)
            act[d, rows8(i)] = v * s
            sg[d, rows8(i)] = s * (1.0 + v * (1.0 - s))
            return carry

        lax.fori_loop(0, L, conv, 0)
        part[d] = nn(act[d], sw[d])
        sums[d].scatter()
    for load in loads[4:]:
        load.wait()
    by_lanes(gate, gates)
    by_lanes(cot, cots)

    def gated(i, carry):
        for b in range(B):
            v = gates[b, every(i)]
            g[rows8(i), b * W : (b + 1) * W] = cots[b, every(i)] * v * sigmoid(v)
        return carry

    lax.fori_loop(0, L, gated, 0)
    for d in range(2):
        for n in range(N):
            rt[d, n] = jnp.broadcast_to(-jnp.exp(dl[d, n : n + 1]) * LOG2E, (C, E))
    for d in range(2):
        sums[d].gather()
    H = 8
    for d in range(2):
        sums[d].wait()
        pre[d] = nn(proj[d][:, :R], stw[d]) + stb[d : d + 1]

        def prepare(i, carry, d=d):
            st = softplus(pre[d, rows8(i)])
            step[d, rows8(i)] = st
            drv[d, rows8(i)] = st * act[d, rows8(i)]
            block = proj[d, rows8(i)]
            for n in range(N):
                inb[d, i, n] = jnp.broadcast_to(block[:, R + n : R + n + 1], (C, W))
                outb[d, i, n] = jnp.broadcast_to(block[:, R + N + n : R + N + n + 1], (C, W))
            return carry

        lax.fori_loop(0, L, prepare, 0)
        up, down = (cu, cd) if d == 0 else (cd, cu)
        for half in range(N // H):

            def ends(c, carry, d=d, half=half, up=up, down=down):
                lanes = pl.ds(pl.multiple_of(c * W, W), W)

                def advance(i, state):
                    f, p, a = state
                    ii = i if d == 0 else L - 1 - i
                    st, dr = step[d, rows8(ii), lanes], drv[d, rows8(ii), lanes]
                    gg = g[rows8(ii), lanes]
                    nf, np_, na = [], [], []
                    for j in range(H):
                        n = half * H + j
                        e = jnp.exp2(st * rt[d, n, :, lanes])
                        dec[d, ii, n, :, lanes] = e
                        nf.append(e * f[j] + inb[d, ii, n] * dr)
                        v = p[j] * e
                        np_.append(v)
                        na.append(a[j] + v * (outb[d, ii, n] * gg))
                    return nf, np_, na

                zero = [jnp.zeros((C, W), F32)] * H
                f, p, a = lax.fori_loop(0, L, advance, (zero, [jnp.ones((C, W), F32)] * H, zero), unroll=UNROLL)
                for j in range(H):
                    n = half * H + j
                    row = rows8(d * 12 + (n % 2) * B + c)
                    up[n // 2, row] = f[j]
                    cp[n // 2, row] = p[j]
                    down[n // 2, row] = a[j]
                return carry

            lax.fori_loop(0, B, ends, 0)

    def totals(q, carry):
        for k in range(3):
            u = dn = jnp.zeros((C, W), F32)
            pt = jnp.ones((C, W), F32)
            for s in range(C):
                at = pl.ds(k * 64 + s, C, stride=C)
                p = cp[q, at]
                u = p * u + cu[q, at]
                pt = pt * p
                back = pl.ds(k * 64 + C - 1 - s, C, stride=C)
                dn = cp[q, back] * dn + cd[q, back]
            msg[q, k * 8 : k * 8 + 8] = u
            msg[q, 24 + k * 8 : 32 + k * 8] = dn
            msg[q, 48 + k * 8 : 56 + k * 8] = pt
        return carry

    lax.fori_loop(0, 8, totals, 0)
    exchange_carries(links, place, msg, cr1, ctot, cr2, czs, czr, cout, crc)

    def starts(q, carry):
        for k in range(3):
            u, dn = crc[q, k * 8 : k * 8 + 8], crc[q, 24 + k * 8 : 32 + k * 8]
            for s in range(C):
                at = pl.ds(k * 64 + s, C, stride=C)
                su[q, at] = u
                u = cp[q, at] * u + cu[q, at]
                back = pl.ds(k * 64 + C - 1 - s, C, stride=C)
                sd[q, back] = dn
                dn = cp[q, back] * dn + cd[q, back]
        return carry

    lax.fori_loop(0, 8, starts, 0)
    Q = 3
    QW = Q * W
    lane = lax.broadcasted_iota(jnp.int32, (C, W), 1)

    def folded(v):
        r = v[:, :W]
        for k in range(1, Q):
            r = r + v[:, k * W : (k + 1) * W]
        return r

    def wide(v):
        return jnp.concatenate([v] * Q, axis=1)

    def begin(src, d, half, cb, j):
        n = half * H + j
        row = d * 12 + (n % 2) * B + cb * Q
        return jnp.concatenate([src[n // 2, pl.ds((row + k) * 8, 8)] for k in range(Q)], axis=1)

    blocks = [(half, cb) for half in range(N // H) for cb in range(B // Q)]

    def sweep(d):
        fs, bs = (su, sd) if d == 0 else (sd, su)
        for half, cb in blocks:
            lanes = pl.ds(cb * QW, QW)

            def forward(i, state, half=half, cb=cb, lanes=lanes):
                ii = i if d == 0 else L - 1 - i
                dr, gg = drv[d, rows8(ii), lanes], g[rows8(ii), lanes]
                if half == 0:
                    y = skip[d : d + 1, lanes] * act[d, rows8(ii), lanes]
                    if d == 1:
                        y = y + ya[rows8(ii), lanes]
                else:
                    y = ya[rows8(ii), lanes]
                new = []
                for j in range(H):
                    n = half * H + j
                    s = dec[d, ii, n, :, lanes] * state[j] + wide(inb[d, ii, n]) * dr
                    y = y + wide(outb[d, ii, n]) * s
                    v = folded(s * gg)
                    go[ii, n] = v if cb == 0 else go[ii, n] + v
                    ss[i + 1, j] = s
                    new.append(s)
                ya[rows8(ii), lanes] = y
                return new

            first = [begin(fs, d, half, cb, j) for j in range(H)]
            for j in range(H):
                ss[0, j] = first[j]
            lax.fori_loop(0, L, forward, first)

            def retreat(t, carried, half=half, cb=cb, lanes=lanes):
                i = L - 1 - t
                ii = i if d == 0 else L - 1 - i
                dr, gg = drv[d, rows8(ii), lanes], g[rows8(ii), lanes]
                if half == 0:
                    a1 = a2 = jnp.zeros((C, QW), F32)
                else:
                    a1, a2 = stt[rows8(ii), lanes], dg[rows8(ii), lanes]
                new = []
                for j in range(H):
                    n = half * H + j
                    adj = carried[j] + wide(outb[d, ii, n]) * gg
                    back = dec[d, ii, n, :, lanes] * adj
                    a1 = a1 + (back * ss[i, j]) * rt[d, n, :, lanes]
                    a2 = a2 + adj * wide(inb[d, ii, n])
                    v = folded(adj * dr)
                    gi[ii, n] = v if cb == 0 else gi[ii, n] + v
                    new.append(back)
                stt[rows8(ii), lanes] = a1
                dg[rows8(ii), lanes] = a2
                return new

            lax.fori_loop(0, L, retreat, [begin(bs, d, half, cb, j) for j in range(H)])

        def close(i, carry):
            at = rows8(i)
            slope = dg[at]
            ga = g[at] * skip[d : d + 1] + slope * step[d, at]
            stt[at] = (stt[at] * LN2 + slope * act[d, at]) * sigmoid(pre[d, at])
            drv[d, at] = ga
            return carry

        lax.fori_loop(0, L, close, 0)
        wpad[0:R] = stw[d]
        part2[d] = nt(stt[...], wpad[...])

        def bases(i, carry):
            v = part2[d, rows8(i)]
            for n in range(N):
                v = v + jnp.where(lane == R + n, jnp.sum(gi[i, n], axis=1, keepdims=True), 0.0)
                v = v + jnp.where(lane == R + N + n, jnp.sum(go[i, n], axis=1, keepdims=True), 0.0)
            part2[d, rows8(i)] = v
            return carry

        lax.fori_loop(0, L, bases, 0)

    wpad[...] = jnp.zeros_like(wpad)
    back_sums = [ChannelSum(links, part2.at[d], landed2.at[d], own2.at[d], gp.at[d], me, ctx) for d in range(2)]
    weights = [
        TileSum(links, place, *[r.at[k] for r in (w_src, w_r0, w_t0, w_r1, w_t2, w_r3, w_t3, w_t4, w_fin)])
        for k in range(4)
    ]
    s0, s1, t0, t1 = weights

    def step_part(d, stream):
        v = tn(proj[d], stt[...])
        for b in range(B):
            stream.src[b * W : (b + 1) * W] = v[:, b * W : (b + 1) * W]

    def select_part(d, stream, ext):
        stream.src[...] = tn(act[d], gp[d])
        stream.core()
        tgp[...] = nt(gp[d], sw[d])

        def conv_grad(i, carry):
            ext[3 + i] = (drv[d, rows8(i)] + tgp[rows8(i)]) * sg[d, rows8(i)]
            return carry

        lax.fori_loop(0, L, conv_grad, 0)

    def step_end(d):
        def write(core, src):
            for b in range(3):
                lanes = pl.ds(pl.multiple_of(core * 384 + b * W, W), W)
                stepg_o[d, :, lanes] = src[b * W : b * W + R]

        return write

    def select_end(d):
        def write(core, src):
            selg_o[d, rows(core, 384)] = src[...]

        return write

    sweep(0)
    back_sums[0].scatter()
    step_part(0, s0)
    s0.core()
    sweep(1)
    back_sums[1].scatter()
    back_sums[0].gather()
    step_part(1, s1)
    s1.core()
    s0.scatter()
    back_sums[0].wait()
    select_part(0, t0, ext0)
    back_sums[1].gather()
    s0.far()
    s1.scatter()
    t0.scatter()
    back_sums[1].wait()
    select_part(1, t1, ext1)
    for k in range(3):
        send0[k : k + 1] = ext0[3 + k, 0:1]
        send1[k : k + 1] = ext1[3 + L - 3 + k, C - 1 : C]
    halo = [links.start(send0, nxt2, place.before), links.start(send1, prev2, place.after)]
    s0.gather()
    t1.scatter()
    s1.far()
    t0.far()

    def gates_back(i, carry):
        for b in range(B):
            v, ct, y = gates[b, every(i)], cots[b, every(i)], ya[rows8(i), b * W : (b + 1) * W]
            s = sigmoid(v)
            gates[b, every(i)] = y * v * s
            cots[b, every(i)] = ct * y * (s * (1.0 + v * (1.0 - s)))
        return carry

    lax.fori_loop(0, L, gates_back, 0)
    for b in range(B):
        out_o[:, b * W : (b + 1) * W] = gates[b]
        gg_o[:, b * W : (b + 1) * W] = cots[b]
    s0.join()
    t1.far()
    s1.gather()
    t0.gather()
    arrived(halo)
    fill_edges(ext0, prev2[0:3], nxt2[0:3], ctx > 0, ctx < TILES - 1)
    fill_edges(ext1, prev2[0:3], nxt2[0:3], ctx > 0, ctx < TILES - 1)

    def conv_back(i, carry):
        v = jnp.zeros((C, E), F32)
        for k in range(4):
            v = v + cw[0, k : k + 1] * ext0[i + 6 - k] + cw[1, k : k + 1] * ext1[i + k]
        for b in range(B):
            tiles[b, every(i)] = v[:, b * W : (b + 1) * W]
        return carry

    lax.fori_loop(0, L, conv_back, 0)
    for b in range(B):
        tg_o[:, b * W : (b + 1) * W] = tiles[b]
    t1.gather()
    s1.join()
    t0.join()
    s0.end(step_end(0))
    t1.join()
    s1.end(step_end(1))
    t0.end(select_end(0))
    t1.end(select_end(1))
    links.finish()


UNROLL = 2


def on_device(*args):
    v = lambda *shape: pltpu.VMEM(shape, F32)
    chunks = v(8, 192, W)
    copies = 2 + 12 + 18 + 12 + 2 + 4 * 33
    any_ = pl.BlockSpec(memory_space=pl.ANY)
    return pl.pallas_call(
        block_kernel,
        out_shape=(sds(T, E), sds(T, E), sds(T, E), sds(2, E, W), sds(2, R, E)),
        in_specs=[any_] * 10,
        out_specs=(VM,) * 5,
        scratch_shapes=[
            v(T, E), v(T, E), v(T, E), v(2, 4, E), v(2, E), v(2, E, W), v(2, R, E), v(2, E), v(2, N, E), v(2, E),
            pltpu.SemaphoreType.DMA((10,)),
            v(B, T, W), v(B, T, W), v(B, T, W), v(8, E), v(8, E), v(8, E), v(8, E), v(8, E), v(8, E),
            v(L + 6, C, E), v(L + 6, C, E),
            v(2, T, E), v(2, T, E), v(2, T, W), v(2, 3, 32, W), v(2, 32, W), v(2, T, W),
            v(2, T, W), v(2, 3, 32, W), v(2, 32, W), v(2, T, W),
            v(2, T, E), v(2, T, E), v(2, T, E), v(T, E), v(2, N, C, E), v(2, L, N, C, W), v(2, L, N, C, W),
            v(2, L, N, C, E), chunks, chunks, chunks, chunks, chunks,
            v(8, 72, W), v(8, 72, W), v(72, W), v(4, 72, W), v(24, W), v(24, W), v(8, 48, W), v(8, 48, W),
            v(L + 1, 8, C, 3 * W), v(L, N, C, W), v(L, N, C, W), v(T, E), v(T, E), v(T, E), v(W, E), v(T, E),
            v(4, E, W), v(4, 384, W), v(4, 384, W), v(4, 15, 24, W), v(4, 24, W), v(4, 24, W), v(4, 24, W),
            v(4, 384, W), v(4, 384, W),
            pltpu.SemaphoreType.DMA((copies,)),
            pltpu.SemaphoreType.DMA((copies,)),
        ],
        compiler_params=pltpu.CompilerParams(
            collective_id=0, has_side_effects=True, vmem_limit_bytes=60 << 20
        ),
        name="block",
    )(*args)


def solution(mesh):
    row = P("ctx", "ch")
    in_specs = (
        row,
        row,
        row,
        P(None, None, "ch"),
        P(None, "ch"),
        P(None, "ch", None),
        P(None, None, "ch"),
        P(None, "ch"),
        P(None, None, "ch"),
        P(None, "ch"),
    )
    out_specs = (row, row, row, P(None, "ch", None), P(None, None, "ch"))
    return jax.shard_map(on_device, mesh=mesh, in_specs=in_specs, out_specs=out_specs, check_vma=False)
```

time: 137 us -> 113 us (0.82)
  Pallas kernels: 126 us -> 107 us
  local copies, waits for them, and re-layouts: 9.68 us -> 5.5 us
    pallas_call x5 -> x1, Pallas kernels: 126 us -> 107 us  [on_device(): pl.pallas_call(block_kernel, out_shape=(sds(T, E), sds(T, E), sds(T, E),...]
    unnamed x35 -> x13, local copies, waits for them, and re-layouts: 9.68 us -> 5.5 us
where the time goes in v1:
time: 113 us
  Pallas kernels  107 us (95%)
  local copies, waits for them, and re-layouts  5.5 us (5%)
    pallas_call x1, Pallas kernels, on_device(): pl.pallas_call(block_kernel, out_shape=(sds(T, E), sds(T, E), sds(T, E),...  107 us
    unnamed x13, local copies, waits for them, and re-layouts  5.5 us

profile of v1, /device:TPU:1, one launch (start us, length us, event | category | flops | bytes accessed | tf_op | source)
XLA Modules:
  0.0 113.1 jit_solution(7892173149751750132)
XLA Ops:
  0.6 107.0 %block.1 = (f32[128,768]{1,0:T(8,128)}, f32[128,768]{1,0:T(8,128)}, f32[128,768]{1,0:T(8,128)}, f32[2,768,128]{2,1,0:T(8,128)}, f32[2,96,768]{2,1,0:T(8,128)}) custom-call(f32[128,768]{1,0:T(8,128)} %tok_h.1, f32[128,768]{1,0:T(8,128)} %gate_h.1, f32[128,768]{1,0:T(8,128)} %cot_h.1, f32[2,4,768]{2,1,0:T(4,128)} %cw_h.1, f32[2,768]{1,0:T(2,128)} %cb_h.1, ...), custom_call_target="tpu_custom_call" | custom-call | tf_op jit(solution)/shard_map/block/pallas_call | solution.py:618
  107.6 0.0 copy-start.3
  107.6 0.0 copy-start.2
  107.6 1.8 %copy.20 = f32[128,768]{1,0:T(8,128)} copy(f32[128,768]{1,0:T(8,128)} %get-tuple-element.10) | data formatting | bytes 786432
  109.5 0.0 copy-done.3
  109.5 0.0 copy-start
  109.5 0.7 copy.21
  110.2 0.0 copy-done.2
  110.2 0.7 copy.22
  111.0 0.0 copy-done
  111.0 0.0 copy-start.1
  111.0 0.9 copy.23
  111.9 0.5 copy-done.1
  112.3 0.8 copy.24
Async XLA Ops:
  107.6 1.9 %copy-start.3 = (f32[128,768]{1,0:T(8,128)S(1)}, f32[128,768]{1,0:T(8,128)}, u32[]{:S(2)}) copy-start(f32[128,768]{1,0:T(8,128)} %get-tuple-element.11) | copy-start | bytes 1179652
  107.6 2.6 %copy-start.2 = (f32[128,768]{1,0:T(8,128)S(1)}, f32[128,768]{1,0:T(8,128)}, u32[]{:S(2)}) copy-start(f32[128,768]{1,0:T(8,128)} %get-tuple-element.12) | copy-start | bytes 1179652
  109.5 1.5 %copy-start = (f32[2,768,128]{2,1,0:T(8,128)S(1)}, f32[2,768,128]{2,1,0:T(8,128)}, u32[]{:S(2)}) copy-start(f32[2,768,128]{2,1,0:T(8,128)} %get-tuple-element.13) | copy-start | bytes 2359300
  111.0 1.3 %copy-start.1 = (f32[2,96,768]{2,1,0:T(8,128)S(1)}, f32[2,96,768]{2,1,0:T(8,128)}, u32[]{:S(2)}) copy-start(f32[2,96,768]{2,1,0:T(8,128)} %get-tuple-element.14) | copy-start | bytes 1769476

commit v2 on v1

--- a/solution.py
+++ b/solution.py
@@ -6,7 +6,6 @@
 from jax.sharding import PartitionSpec as P
 
 F32 = jnp.float32
-HIGH = lax.Precision.HIGHEST
 MESH = pl.DeviceIdType.MESH
 
 T = 128
@@ -42,16 +41,30 @@
     return pl.ds(pl.multiple_of(i * 8, 8), 8)
 
 
+def parts(a):
+    high = a.astype(jnp.bfloat16)
+    return high, (a - high.astype(F32)).astype(jnp.bfloat16)
+
+
+def product(a, b, left, right):
+    (ah, al), (bh, bl) = parts(a), parts(b)
+
+    def dot(u, v):
+        return lax.dot_general(u, v, (((left,), (right,)), ((), ())), preferred_element_type=F32)
+
+    return dot(ah, bh) + (dot(ah, bl) + dot(al, bh))
+
+
 def nn(a, b):
-    return lax.dot_general(a, b, (((1,), (0,)), ((), ())), precision=HIGH, preferred_element_type=F32)
+    return product(a, b, 1, 0)
 
 
 def nt(a, b):
-    return lax.dot_general(a, b, (((1,), (1,)), ((), ())), precision=HIGH, preferred_element_type=F32)
+    return product(a, b, 1, 1)
 
 
 def tn(a, b):
-    return lax.dot_general(a, b, (((0,), (0,)), ((), ())), precision=HIGH, preferred_element_type=F32)
+    return product(a, b, 0, 0)
 
 
 class Links:
@@ -84,11 +97,11 @@
         copy.wait_recv()
 
 
-def greet(devices):
+def hail(devices):
     barrier = pltpu.get_barrier_semaphore()
     for device in devices:
         pl.semaphore_signal(barrier, inc=1, device_id=device, device_id_type=MESH)
-    pl.semaphore_wait(barrier, len(devices))
+    return lambda: pl.semaphore_wait(barrier, len(devices))
 
 
 def plus(a, p, n):
@@ -192,7 +205,7 @@
         self.ctx, self.me = ctx, me
         self.after, self.before = (plus(ctx, 1, TILES), me), (plus(ctx, TILES - 1, TILES), me)
         self.core, self.y, self.x = lax.rem(ctx, 2), lax.rem(ctx // 2, 4), lax.rem(ctx // 8, 4)
-        self.q, self.z = lax.rem(ctx, 8), ctx // 32
+        self.z = ctx // 32
         self.mate = (ctx - self.core + 1 - self.core, me)
         self.far = (lax.rem(ctx + 32, TILES), me)
         self.k = self.x * 4 + self.y
@@ -202,55 +215,62 @@
                 if dx or dy:
                     x, y = plus(self.x, dx, 4), plus(self.y, dy, 4)
                     self.plane.append((x * 4 + y, (ctx + (x - self.x) * 8 + (y - self.y) * 2, me)))
-        base = ctx - self.q
-        self.near = [(k, (base + k, me)) for k in [plus(self.q, p, 8) for p in range(1, 8)]]
-        self.across = [(ctx + (plus(self.x, p, 4) - self.x) * 8, me) for p in range(1, 4)]
+        self.k32 = lax.rem(ctx, 32)
+        base = ctx - self.k32
+        self.half = [(k, (base + k, me)) for k in [plus(self.k32, p, 32) for p in range(1, 32)]]
         self.ch = [(ctx, plus(me, p, 4)) for p in range(1, 4)]
 
     def everyone(self):
-        plane = [dev for _, dev in self.plane]
-        return [self.after, self.before, self.far] + plane + [dev for _, dev in self.near] + self.ch
-
-
-def exchange_carries(links, place, msg, r1, tot, r2, zs, zr, out, rc):
-    q, x, z = place.q, place.x, place.z
-    copies = [links.start(msg.at[k], r1.at[q], dev) for k, dev in place.near]
-    r1[q] = msg[q]
-    arrived(copies)
-
-    def fold(buf, count, u, dn):
-        pt = None
-        for s in range(count):
-            u = buf[s, 48:72] * u + buf[s, 0:24]
-            b = count - 1 - s
-            dn = buf[b, 48:72] * dn + buf[b, 24:48]
-            pt = buf[s, 48:72] if pt is None else pt * buf[s, 48:72]
-        return u, dn, pt
-
-    zero = jnp.zeros((24, W), F32)
-    u, dn, pt = fold(r1, 8, zero, zero)
-    tot[0:24], tot[24:48], tot[48:72] = u, dn, pt
-    copies = [links.start(tot, r2.at[x], dev) for dev in place.across]
-    r2[x] = tot[...]
-    arrived(copies)
-    u, dn, pt = fold(r2, 4, zero, zero)
-    zs[...] = jnp.where(z == 0, u, dn)
-    arrived([links.start(zs, zr, place.far)])
-    got = zr[...]
-    u, dn = jnp.where(z == 1, got, 0.0), jnp.where(z == 0, got, 0.0)
-    for s in range(4):
-        u = jnp.where(s < x, r2[s, 48:72] * u + r2[s, 0:24], u)
-        b = 3 - s
-        dn = jnp.where(b > x, r2[b, 48:72] * dn + r2[b, 24:48], dn)
-    for s in range(8):
-        out[s, 0:24] = u
-        u = r1[s, 48:72] * u + r1[s, 0:24]
-        b = 7 - s
-        out[b, 24:48] = dn
-        dn = r1[b, 48:72] * dn + r1[b, 24:48]
-    copies = [links.start(out.at[k], rc.at[q], dev) for k, dev in place.near]
-    rc[q] = out[q]
-    arrived(copies)
+        return [self.after, self.before, self.far] + [dev for _, dev in self.half] + self.ch
+
+
+class Carries:
+    def __init__(self, links, place, d, msg, r1, zs, zr, out, rc):
+        self.links, self.place, self.d = links, place, d
+        self.msg, self.r1, self.zs, self.zr, self.out, self.rc = msg, r1, zs, zr, out, rc
+
+    def pick(self, up, down):
+        sub = lax.broadcasted_iota(jnp.int32, (C, W), 0)
+        return jnp.where(sub < 3, up, down) if self.d == 0 else jnp.where(sub < 3, down, up)
+
+    def start(self):
+        me = self.place.k32
+        self.copies = [self.links.start(self.msg.at[k], self.r1.at[me], dev) for k, dev in self.place.half]
+        self.r1[me] = self.msg[me]
+
+    def far(self):
+        arrived(self.copies)
+        r1 = self.r1
+        u = dn = jnp.zeros((C, W), F32)
+        for s in range(32):
+            u = r1[s, 8:16] * u + r1[s, 0:8]
+            dn = r1[31 - s, 8:16] * dn + r1[31 - s, 0:8]
+        self.zs[...] = self.pick(u, dn)
+        self.copies = [self.links.start(self.zs, self.zr, self.place.far)]
+
+    def back(self):
+        arrived(self.copies)
+        got, z, r1, out = self.zr[...], self.place.z, self.r1, self.out
+        u, dn = jnp.where(z == 1, got, 0.0), jnp.where(z == 0, got, 0.0)
+        ups, downs = [], []
+        for s in range(32):
+            ups.append(u)
+            u = r1[s, 8:16] * u + r1[s, 0:8]
+            if s < 16:
+                out[s] = ups[s]
+            downs.append(dn)
+            dn = r1[31 - s, 8:16] * dn + r1[31 - s, 0:8]
+            if s < 16:
+                out[31 - s] = downs[s]
+            else:
+                out[s] = self.pick(ups[s], out[s])
+                out[31 - s] = self.pick(out[31 - s], downs[s])
+        me = self.place.k32
+        self.copies = [self.links.start(out.at[k], self.rc.at[me], dev) for k, dev in self.place.half]
+        self.rc[me] = out[me]
+
+    def wait(self):
+        arrived(self.copies)
 
 
 def block_kernel(
@@ -259,40 +279,37 @@
     tok, gate, cot, cw, cb, sw, stw, stb, dl, skip, in_sem,
     tiles, gates, cots, prev, nxt, prev2, nxt2, send0, send1, ext0, ext1,
     act, sg, part, landed, own, proj, part2, landed2, own2, gp,
-    pre, step, drv, g, rt, inb, outb, dec, cu, cd, cp, su, sd,
-    msg, cr1, ctot, cr2, czs, czr, cout, crc,
-    ss, go, gi, ya, dg, stt, wpad, tgp,
+    pre, step, drv, g, rt, base, lift, dec, ca, cp, su, sd,
+    msg, cr1, czs, czr, cout, crc,
+    ss, go, gi, pick, ya, dg, stt, wpad, tgp,
     w_src, w_r0, w_t0, w_r1, w_t2, w_r3, w_t3, w_t4, w_fin,
     send, recv,
 ):
     pairs = (
-        (tok_h, tok), (cw_h, cw), (cb_h, cb), (sw_h, sw), (gate_h, gate), (cot_h, cot),
-        (stw_h, stw), (stb_h, stb), (dl_h, dl), (skip_h, skip),
+        (tok_h, tok), (cw_h, cw), (cb_h, cb), (gate_h, gate), (cot_h, cot), (dl_h, dl),
+        (sw_h, sw), (stw_h, stw), (stb_h, stb), (skip_h, skip),
     )
     loads = [pltpu.make_async_copy(a, b, in_sem.at[k]) for k, (a, b) in enumerate(pairs)]
     for load in loads:
         load.start()
     place = Place()
     ctx, me = place.ctx, place.me
-    greet(place.everyone())
+    meet = hail(place.everyone())
+    meet()
     links = Links(send, recv)
     halo = [
         links.start(tok_h.at[pl.ds(T - 8, 8)], prev, place.after),
         links.start(tok_h.at[pl.ds(0, 8)], nxt, place.before),
     ]
-    loads[0].wait()
+    for load in loads[:3]:
+        load.wait()
     by_lanes(tok, tiles)
     for i in range(L):
         for b in range(B):
             ext0[3 + i, :, b * W : (b + 1) * W] = tiles[b, every(i)]
-    for load in loads[1:4]:
-        load.wait()
-    arrived(halo)
-    fill_edges(ext0, prev[5:8], nxt[0:3], ctx > 0, ctx < TILES - 1)
-    sums = [ChannelSum(links, part.at[d], landed.at[d], own.at[d], proj.at[d], me, ctx) for d in range(2)]
-    for d in range(2):
-
-        def conv(i, carry, d=d):
+
+    def conv(d):
+        def one(i, carry):
             v = jnp.broadcast_to(cb[d : d + 1], (C, E))
             for k in range(4):
                 v = v + cw[d, k : k + 1] * ext0[i + (k if d == 0 else 6 - k)]
@@ -301,10 +318,11 @@
             sg[d, rows8(i)] = s * (1.0 + v * (1.0 - s))
             return carry
 
-        lax.fori_loop(0, L, conv, 0)
-        part[d] = nn(act[d], sw[d])
-        sums[d].scatter()
-    for load in loads[4:]:
+        return one
+
+    lax.fori_loop(3, L, conv(0), 0)
+    lax.fori_loop(0, L - 3, conv(1), 0)
+    for load in loads[3:]:
         load.wait()
     by_lanes(gate, gates)
     by_lanes(cot, cots)
@@ -315,32 +333,53 @@
             g[rows8(i), b * W : (b + 1) * W] = cots[b, every(i)] * v * sigmoid(v)
         return carry
 
-    lax.fori_loop(0, L, gated, 0)
+    lax.fori_loop(0, L, gated, 0, unroll=2)
     for d in range(2):
+        ca[d, :, 48:64] = jnp.zeros((32, 16, W), F32)
+        cp[d, :, 48:64] = jnp.zeros((32, 16, W), F32)
         for n in range(N):
             rt[d, n] = jnp.broadcast_to(-jnp.exp(dl[d, n : n + 1]) * LOG2E, (C, E))
+    lane = lax.broadcasted_iota(jnp.int32, (W, W), 1)
+    line = lax.broadcasted_iota(jnp.int32, (W, W), 0)
+    for n in range(2 * N):
+        at = pl.ds(n * W, W)
+        pick[at] = jnp.where(lane == R + n, 1.0, 0.0).astype(jnp.bfloat16)
+        lift[0:W, at] = jnp.where(line == R + n, 1.0, 0.0).astype(jnp.bfloat16)
+        lift[W : 2 * W, at] = jnp.where(line == R + n, 1.0, 0.0).astype(jnp.bfloat16)
+    arrived(halo)
+    fill_edges(ext0, prev[5:8], nxt[0:3], ctx > 0, ctx < TILES - 1)
+    sums = [ChannelSum(links, part.at[d], landed.at[d], own.at[d], proj.at[d], me, ctx) for d in range(2)]
+    lax.fori_loop(0, 3, conv(0), 0)
+    part[0] = nn(act[0], sw[0])
+    sums[0].scatter()
+    lax.fori_loop(L - 3, L, conv(1), 0)
+    part[1] = nn(act[1], sw[1])
+    sums[1].scatter()
     for d in range(2):
         sums[d].gather()
+    def basis(d, i, n):
+        return base[d, rows8(i), n * W : (n + 1) * W]
+
     H = 8
+    carries = [Carries(links, place, d, *[r.at[d] for r in (msg, cr1, czs, czr, cout, crc)]) for d in range(2)]
     for d in range(2):
         sums[d].wait()
+        spread = jnp.concatenate(parts(proj[d]), axis=1)
+        for n in range(0, 2 * N, 2):
+            at = pl.ds(n * W, 2 * W)
+            base[d, :, at] = jnp.dot(spread, lift[:, at], preferred_element_type=F32)
         pre[d] = nn(proj[d][:, :R], stw[d]) + stb[d : d + 1]
 
         def prepare(i, carry, d=d):
             st = softplus(pre[d, rows8(i)])
             step[d, rows8(i)] = st
             drv[d, rows8(i)] = st * act[d, rows8(i)]
-            block = proj[d, rows8(i)]
-            for n in range(N):
-                inb[d, i, n] = jnp.broadcast_to(block[:, R + n : R + n + 1], (C, W))
-                outb[d, i, n] = jnp.broadcast_to(block[:, R + N + n : R + N + n + 1], (C, W))
             return carry
 
-        lax.fori_loop(0, L, prepare, 0)
-        up, down = (cu, cd) if d == 0 else (cd, cu)
+        lax.fori_loop(0, L, prepare, 0, unroll=PREP)
         for half in range(N // H):
 
-            def ends(c, carry, d=d, half=half, up=up, down=down):
+            def ends(c, carry, d=d, half=half):
                 lanes = pl.ds(pl.multiple_of(c * W, W), W)
 
                 def advance(i, state):
@@ -353,59 +392,48 @@
                         n = half * H + j
                         e = jnp.exp2(st * rt[d, n, :, lanes])
                         dec[d, ii, n, :, lanes] = e
-                        nf.append(e * f[j] + inb[d, ii, n] * dr)
+                        nf.append(e * f[j] + basis(d, ii, n) * dr)
                         v = p[j] * e
                         np_.append(v)
-                        na.append(a[j] + v * (outb[d, ii, n] * gg))
+                        na.append(a[j] + v * (basis(d, ii, N + n) * gg))
                     return nf, np_, na
 
                 zero = [jnp.zeros((C, W), F32)] * H
                 f, p, a = lax.fori_loop(0, L, advance, (zero, [jnp.ones((C, W), F32)] * H, zero), unroll=UNROLL)
                 for j in range(H):
                     n = half * H + j
-                    row = rows8(d * 12 + (n % 2) * B + c)
-                    up[n // 2, row] = f[j]
-                    cp[n // 2, row] = p[j]
-                    down[n // 2, row] = a[j]
+                    slot = n * 2 + c // 3
+                    first, second = rows8(lax.rem(c, 3)), rows8(lax.rem(c, 3) + 3)
+                    ca[d, slot, first] = f[j]
+                    ca[d, slot, second] = a[j]
+                    cp[d, slot, first] = p[j]
+                    cp[d, slot, second] = p[j]
                 return carry
 
             lax.fori_loop(0, B, ends, 0)
 
-    def totals(q, carry):
-        for k in range(3):
+        def totals(q, carry, d=d):
             u = dn = jnp.zeros((C, W), F32)
             pt = jnp.ones((C, W), F32)
             for s in range(C):
-                at = pl.ds(k * 64 + s, C, stride=C)
-                p = cp[q, at]
-                u = p * u + cu[q, at]
+                p, back = cp[d, q, pl.ds(s, C, stride=C)], pl.ds(C - 1 - s, C, stride=C)
+                u = p * u + ca[d, q, pl.ds(s, C, stride=C)]
                 pt = pt * p
-                back = pl.ds(k * 64 + C - 1 - s, C, stride=C)
-                dn = cp[q, back] * dn + cd[q, back]
-            msg[q, k * 8 : k * 8 + 8] = u
-            msg[q, 24 + k * 8 : 32 + k * 8] = dn
-            msg[q, 48 + k * 8 : 56 + k * 8] = pt
-        return carry
-
-    lax.fori_loop(0, 8, totals, 0)
-    exchange_carries(links, place, msg, cr1, ctot, cr2, czs, czr, cout, crc)
-
-    def starts(q, carry):
-        for k in range(3):
-            u, dn = crc[q, k * 8 : k * 8 + 8], crc[q, 24 + k * 8 : 32 + k * 8]
-            for s in range(C):
-                at = pl.ds(k * 64 + s, C, stride=C)
-                su[q, at] = u
-                u = cp[q, at] * u + cu[q, at]
-                back = pl.ds(k * 64 + C - 1 - s, C, stride=C)
-                sd[q, back] = dn
-                dn = cp[q, back] * dn + cd[q, back]
-        return carry
-
-    lax.fori_loop(0, 8, starts, 0)
+                dn = cp[d, q, back] * dn + ca[d, q, back]
+            msg[d, q, 0:8] = carries[d].pick(u, dn)
+            msg[d, q, 8:16] = pt
+            return carry
+
+        lax.fori_loop(0, 32, totals, 0, unroll=4)
+        if d == 0:
+            carries[0].start()
+    carries[0].far()
+    carries[0].back()
+    carries[1].start()
+    carries[0].wait()
+
     Q = 3
     QW = Q * W
-    lane = lax.broadcasted_iota(jnp.int32, (C, W), 1)
 
     def folded(v):
         r = v[:, :W]
@@ -416,16 +444,28 @@
     def wide(v):
         return jnp.concatenate([v] * Q, axis=1)
 
-    def begin(src, d, half, cb, j):
+    def begin(src, first, half, cb, j):
         n = half * H + j
-        row = d * 12 + (n % 2) * B + cb * Q
-        return jnp.concatenate([src[n // 2, pl.ds((row + k) * 8, 8)] for k in range(Q)], axis=1)
+        return jnp.concatenate([src[n * 2 + cb, pl.ds((first + k) * 8, 8)] for k in range(Q)], axis=1)
 
     blocks = [(half, cb) for half in range(N // H) for cb in range(B // Q)]
 
-    def sweep(d):
+    def sweep(d, between):
+        def starts(q, carry):
+            u = dn = crc[d, q]
+            for s in range(C):
+                at, back = pl.ds(s, C, stride=C), pl.ds(C - 1 - s, C, stride=C)
+                su[q, at] = u
+                u = cp[d, q, at] * u + ca[d, q, at]
+                sd[q, back] = dn
+                dn = cp[d, q, back] * dn + ca[d, q, back]
+            return carry
+
+        lax.fori_loop(0, 32, starts, 0, unroll=4)
         fs, bs = (su, sd) if d == 0 else (sd, su)
         for half, cb in blocks:
+            for step_on in between.get((half, cb), ()):
+                step_on()
             lanes = pl.ds(cb * QW, QW)
 
             def forward(i, state, half=half, cb=cb, lanes=lanes):
@@ -440,19 +480,19 @@
                 new = []
                 for j in range(H):
                     n = half * H + j
-                    s = dec[d, ii, n, :, lanes] * state[j] + wide(inb[d, ii, n]) * dr
-                    y = y + wide(outb[d, ii, n]) * s
-                    v = folded(s * gg)
-                    go[ii, n] = v if cb == 0 else go[ii, n] + v
+                    s = dec[d, ii, n, :, lanes] * state[j] + wide(basis(d, ii, n)) * dr
+                    y = y + wide(basis(d, ii, N + n)) * s
+                    v, at = folded(s * gg), pl.ds(n * W, W)
+                    go[rows8(ii), at] = v if cb == 0 else go[rows8(ii), at] + v
                     ss[i + 1, j] = s
                     new.append(s)
                 ya[rows8(ii), lanes] = y
                 return new
 
-            first = [begin(fs, d, half, cb, j) for j in range(H)]
+            first = [begin(fs, 0, half, cb, j) for j in range(H)]
             for j in range(H):
                 ss[0, j] = first[j]
-            lax.fori_loop(0, L, forward, first)
+            lax.fori_loop(0, L, forward, first, unroll=SW)
 
             def retreat(t, carried, half=half, cb=cb, lanes=lanes):
                 i = L - 1 - t
@@ -465,18 +505,21 @@
                 new = []
                 for j in range(H):
                     n = half * H + j
-                    adj = carried[j] + wide(outb[d, ii, n]) * gg
+                    adj = carried[j] + wide(basis(d, ii, N + n)) * gg
                     back = dec[d, ii, n, :, lanes] * adj
                     a1 = a1 + (back * ss[i, j]) * rt[d, n, :, lanes]
-                    a2 = a2 + adj * wide(inb[d, ii, n])
-                    v = folded(adj * dr)
-                    gi[ii, n] = v if cb == 0 else gi[ii, n] + v
+                    a2 = a2 + adj * wide(basis(d, ii, n))
+                    v, at = folded(adj * dr), pl.ds(n * W, W)
+                    gi[rows8(ii), at] = v if cb == 0 else gi[rows8(ii), at] + v
                     new.append(back)
                 stt[rows8(ii), lanes] = a1
                 dg[rows8(ii), lanes] = a2
                 return new
 
-            lax.fori_loop(0, L, retreat, [begin(bs, d, half, cb, j) for j in range(H)])
+            lax.fori_loop(0, L, retreat, [begin(bs, 3, half, cb, j) for j in range(H)], unroll=SW)
+
+        for step_on in between["close"]:
+            step_on()
 
         def close(i, carry):
             at = rows8(i)
@@ -490,15 +533,12 @@
         wpad[0:R] = stw[d]
         part2[d] = nt(stt[...], wpad[...])
 
-        def bases(i, carry):
-            v = part2[d, rows8(i)]
-            for n in range(N):
-                v = v + jnp.where(lane == R + n, jnp.sum(gi[i, n], axis=1, keepdims=True), 0.0)
-                v = v + jnp.where(lane == R + N + n, jnp.sum(go[i, n], axis=1, keepdims=True), 0.0)
-            part2[d, rows8(i)] = v
-            return carry
-
-        lax.fori_loop(0, L, bases, 0)
+        total = part2[d]
+        for k in range(0, 2 * N, 4):
+            source = (gi if k < N else go)[:, (k % N) * W : (k % N + 4) * W]
+            for half in parts(source):
+                total = total + jnp.dot(half, pick[k * W : (k + 4) * W], preferred_element_type=F32)
+        part2[d] = total
 
     wpad[...] = jnp.zeros_like(wpad)
     back_sums = [ChannelSum(links, part2.at[d], landed2.at[d], own2.at[d], gp.at[d], me, ctx) for d in range(2)]
@@ -538,32 +578,21 @@
 
         return write
 
-    sweep(0)
+    sweep(0, {(0, 1): [carries[1].far], "close": [carries[1].back]})
     back_sums[0].scatter()
     step_part(0, s0)
     s0.core()
-    sweep(1)
+    carries[1].wait()
+    sweep(1, {(0, 1): [back_sums[0].gather, s0.scatter], "close": [s0.far]})
     back_sums[1].scatter()
-    back_sums[0].gather()
     step_part(1, s1)
     s1.core()
-    s0.scatter()
     back_sums[0].wait()
     select_part(0, t0, ext0)
     back_sums[1].gather()
-    s0.far()
+    s0.gather()
     s1.scatter()
     t0.scatter()
-    back_sums[1].wait()
-    select_part(1, t1, ext1)
-    for k in range(3):
-        send0[k : k + 1] = ext0[3 + k, 0:1]
-        send1[k : k + 1] = ext1[3 + L - 3 + k, C - 1 : C]
-    halo = [links.start(send0, nxt2, place.before), links.start(send1, prev2, place.after)]
-    s0.gather()
-    t1.scatter()
-    s1.far()
-    t0.far()
 
     def gates_back(i, carry):
         for b in range(B):
@@ -573,11 +602,21 @@
             cots[b, every(i)] = ct * y * (s * (1.0 + v * (1.0 - s)))
         return carry
 
-    lax.fori_loop(0, L, gates_back, 0)
+    lax.fori_loop(0, L, gates_back, 0, unroll=2)
     for b in range(B):
         out_o[:, b * W : (b + 1) * W] = gates[b]
         gg_o[:, b * W : (b + 1) * W] = cots[b]
+    back_sums[1].wait()
+    select_part(1, t1, ext1)
+    for k in range(3):
+        send0[k : k + 1] = ext0[3 + k, 0:1]
+        send1[k : k + 1] = ext1[3 + L - 3 + k, C - 1 : C]
+    halo = [links.start(send0, nxt2, place.before), links.start(send1, prev2, place.after)]
+    t1.scatter()
+    s1.far()
+    t0.far()
     s0.join()
+
     t1.far()
     s1.gather()
     t0.gather()
@@ -607,18 +646,31 @@
     links.finish()
 
 
-UNROLL = 2
+UNROLL = 4
+PREP = 2
+SW = 2
+LIMIT = 49 << 20
+
+
+def store_kernel(*refs):
+    ins, outs, sem = refs[:5], refs[5:10], refs[10]
+    copies = [pltpu.make_async_copy(a, b, sem.at[k]) for k, (a, b) in enumerate(zip(ins, outs))]
+    for copy in copies:
+        copy.start()
+    for copy in copies:
+        copy.wait()
 
 
 def on_device(*args):
     v = lambda *shape: pltpu.VMEM(shape, F32)
-    chunks = v(8, 192, W)
-    copies = 2 + 12 + 18 + 12 + 2 + 4 * 33
-    any_ = pl.BlockSpec(memory_space=pl.ANY)
-    return pl.pallas_call(
+    copies = 2 + 12 + 2 * 63 + 12 + 2 + 4 * 33
+    hbm = pl.BlockSpec(memory_space=pltpu.HBM)
+    shapes = (sds(T, E), sds(T, E), sds(T, E), sds(2, E, W), sds(2, R, E))
+    args = [pltpu.with_memory_space_constraint(a, pltpu.HBM) for a in args]
+    results = pl.pallas_call(
         block_kernel,
-        out_shape=(sds(T, E), sds(T, E), sds(T, E), sds(2, E, W), sds(2, R, E)),
-        in_specs=[any_] * 10,
+        out_shape=shapes,
+        in_specs=[hbm] * 10,
         out_specs=(VM,) * 5,
         scratch_shapes=[
             v(T, E), v(T, E), v(T, E), v(2, 4, E), v(2, E), v(2, E, W), v(2, R, E), v(2, E), v(2, N, E), v(2, E),
@@ -627,20 +679,30 @@
             v(L + 6, C, E), v(L + 6, C, E),
             v(2, T, E), v(2, T, E), v(2, T, W), v(2, 3, 32, W), v(2, 32, W), v(2, T, W),
             v(2, T, W), v(2, 3, 32, W), v(2, 32, W), v(2, T, W),
-            v(2, T, E), v(2, T, E), v(2, T, E), v(T, E), v(2, N, C, E), v(2, L, N, C, W), v(2, L, N, C, W),
-            v(2, L, N, C, E), chunks, chunks, chunks, chunks, chunks,
-            v(8, 72, W), v(8, 72, W), v(72, W), v(4, 72, W), v(24, W), v(24, W), v(8, 48, W), v(8, 48, W),
-            v(L + 1, 8, C, 3 * W), v(L, N, C, W), v(L, N, C, W), v(T, E), v(T, E), v(T, E), v(W, E), v(T, E),
+            v(2, T, E), v(2, T, E), v(2, T, E), v(T, E), v(2, N, C, E), v(2, T, 2 * N * W),
+            pltpu.VMEM((2 * W, 2 * N * W), jnp.bfloat16),
+            v(2, L, N, C, E), v(2, 32, 64, W), v(2, 32, 64, W), v(32, 64, W), v(32, 64, W),
+            v(2, 32, 16, W), v(2, 32, 16, W), v(2, C, W), v(2, C, W), v(2, 32, C, W), v(2, 32, C, W),
+            v(L + 1, 8, C, 3 * W), v(T, N * W), v(T, N * W), pltpu.VMEM((2 * N * W, W), jnp.bfloat16), v(T, E), v(T, E), v(T, E), v(W, E), v(T, E),
             v(4, E, W), v(4, 384, W), v(4, 384, W), v(4, 15, 24, W), v(4, 24, W), v(4, 24, W), v(4, 24, W),
             v(4, 384, W), v(4, 384, W),
             pltpu.SemaphoreType.DMA((copies,)),
             pltpu.SemaphoreType.DMA((copies,)),
         ],
         compiler_params=pltpu.CompilerParams(
-            collective_id=0, has_side_effects=True, vmem_limit_bytes=60 << 20
+            collective_id=0, has_side_effects=True, vmem_limit_bytes=LIMIT
         ),
         name="block",
     )(*args)
+    return pl.pallas_call(
+        store_kernel,
+        out_shape=shapes,
+        in_specs=[VM] * 5,
+        out_specs=(hbm,) * 5,
+        scratch_shapes=[pltpu.SemaphoreType.DMA((5,))],
+        compiler_params=pltpu.CompilerParams(vmem_limit_bytes=1 << 20),
+        name="store",
+    )(*results)
 
 
 def solution(mesh):

time: 113 us -> 101 us (0.89)
  Pallas kernels: 107 us -> 99.8 us
  local copies, waits for them, and re-layouts: 5.5 us -> 0 us
    pallas_call x1 -> x2, Pallas kernels: 107 us -> 99.8 us  [the longest x1 98.3 us: on_device(): pl.pallas_call(block_kernel, out_shape=shapes, in_specs=[hbm] * 10, out_s...]
    unnamed x13 -> x0, local copies, waits for them, and re-layouts: 5.5 us -> none
where the time goes in v2:
time: 101 us; the launch traced here: 100 us
  Pallas kernels  99.8 us (99%)
    pallas_call x1, Pallas kernels, on_device(): pl.pallas_call(block_kernel, out_shape=shapes, in_specs=[hbm] * 10, out_s...  98.3 us

profile of v2, /device:TPU:1, one launch (start us, length us, event | category | flops | bytes accessed | tf_op | source)
XLA Modules:
  0.0 100.5 jit_solution(3630327549397618079)
XLA Ops:
  0.6 98.3 %block.1 = (f32[128,768]{1,0:T(8,128)S(1)}, f32[128,768]{1,0:T(8,128)S(1)}, f32[128,768]{1,0:T(8,128)S(1)}, f32[2,768,128]{2,1,0:T(8,128)S(1)}, f32[2,96,768]{2,1,0:T(8,128)S(1)}) custom-call(f32[128,768]{1,0:T(8,128)} %tok_h.1, f32[128,768]{1,0:T(8,128)} %gate_h.1, f32[128,768]{1,0:T(8,128)} %cot_h.1, f32[2,4,768]{2,1,0:T(4,128)} %cw_h.1, f32[2,768]{1,0:T(2,128)} %cb_h.1, ...), custom_call_target="tpu_custom_call" | custom-call | tf_op jit(solution)/shard_map/block/pallas_call | solution.py:670
  99.0 1.5 %store.1 = (f32[128,768]{1,0:T(8,128)}, f32[128,768]{1,0:T(8,128)}, f32[128,768]{1,0:T(8,128)}, f32[2,768,128]{2,1,0:T(8,128)}, f32[2,96,768]{2,1,0:T(8,128)}) custom-call(f32[128,768]{1,0:T(8,128)S(1)} %get-tuple-element.10.refs_0_, f32[128,768]{1,0:T(8,128)S(1)} %get-tuple-element.11.refs_1_, f32[128,768]{1,0:T(8,128)S(1)} %get-tuple-element.12.refs_2_, ...), custom_call_target="tpu_custom_call" | custom-call | tf_op jit(solution)/shard_map/store/pallas_call | solution.py:697

commit v3 on v2

--- a/solution.py
+++ b/solution.py
@@ -399,7 +399,7 @@
                     return nf, np_, na
 
                 zero = [jnp.zeros((C, W), F32)] * H
-                f, p, a = lax.fori_loop(0, L, advance, (zero, [jnp.ones((C, W), F32)] * H, zero), unroll=UNROLL)
+                f, p, a = lax.fori_loop(0, L, advance, (zero, [jnp.ones((C, W), F32)] * H, zero), unroll=UNROLL[d])
                 for j in range(H):
                     n = half * H + j
                     slot = n * 2 + c // 3
@@ -427,10 +427,12 @@
         lax.fori_loop(0, 32, totals, 0, unroll=4)
         if d == 0:
             carries[0].start()
+    carries[1].start()
     carries[0].far()
     carries[0].back()
-    carries[1].start()
+    carries[1].far()
     carries[0].wait()
+    carries[1].back()
 
     Q = 3
     QW = Q * W
@@ -518,9 +520,6 @@
 
             lax.fori_loop(0, L, retreat, [begin(bs, 3, half, cb, j) for j in range(H)], unroll=SW)
 
-        for step_on in between["close"]:
-            step_on()
-
         def close(i, carry):
             at = rows8(i)
             slope = dg[at]
@@ -578,17 +577,18 @@
 
         return write
 
-    sweep(0, {(0, 1): [carries[1].far], "close": [carries[1].back]})
+    sweep(0, {})
     back_sums[0].scatter()
     step_part(0, s0)
     s0.core()
     carries[1].wait()
-    sweep(1, {(0, 1): [back_sums[0].gather, s0.scatter], "close": [s0.far]})
+    sweep(1, {(0, 1): [back_sums[0].gather, s0.scatter]})
     back_sums[1].scatter()
     step_part(1, s1)
     s1.core()
     back_sums[0].wait()
     select_part(0, t0, ext0)
+    s0.far()
     back_sums[1].gather()
     s0.gather()
     s1.scatter()
@@ -646,7 +646,7 @@
     links.finish()
 
 
-UNROLL = 4
+UNROLL = (8, 4)
 PREP = 2
 SW = 2
 LIMIT = 49 << 20

time: 101 us -> 96 us (0.950)
  Pallas kernels: 99.8 us -> 95.2 us
    pallas_call x1, Pallas kernels: 98.3 us -> 93.7 us  [on_device(): pl.pallas_call(block_kernel, out_shape=shapes, in_specs=[hbm] * 10, out_s...]
where the time goes in v3:
time: 96 us; the launch traced here: 95.9 us
  Pallas kernels  95.2 us (99%)
    pallas_call x1, Pallas kernels, on_device(): pl.pallas_call(block_kernel, out_shape=shapes, in_specs=[hbm] * 10, out_s...  93.7 us

profile of v3, /device:TPU:1, one launch (start us, length us, event | category | flops | bytes accessed | tf_op | source)
XLA Modules:
  0.0 95.9 jit_solution(13184033945975789968)
XLA Ops:
  0.6 93.7 %block.1 = (f32[128,768]{1,0:T(8,128)S(1)}, f32[128,768]{1,0:T(8,128)S(1)}, f32[128,768]{1,0:T(8,128)S(1)}, f32[2,768,128]{2,1,0:T(8,128)S(1)}, f32[2,96,768]{2,1,0:T(8,128)S(1)}) custom-call(f32[128,768]{1,0:T(8,128)} %tok_h.1, f32[128,768]{1,0:T(8,128)} %gate_h.1, f32[128,768]{1,0:T(8,128)} %cot_h.1, f32[2,4,768]{2,1,0:T(4,128)} %cw_h.1, f32[2,768]{1,0:T(2,128)} %cb_h.1, ...), custom_call_target="tpu_custom_call" | custom-call | tf_op jit(solution)/shard_map/block/pallas_call | solution.py:670
  94.4 1.5 %store.1 = (f32[128,768]{1,0:T(8,128)}, f32[128,768]{1,0:T(8,128)}, f32[128,768]{1,0:T(8,128)}, f32[2,768,128]{2,1,0:T(8,128)}, f32[2,96,768]{2,1,0:T(8,128)}) custom-call(f32[128,768]{1,0:T(8,128)S(1)} %get-tuple-element.10.refs_0_, f32[128,768]{1,0:T(8,128)S(1)} %get-tuple-element.11.refs_1_, f32[128,768]{1,0:T(8,128)S(1)} %get-tuple-element.12.refs_2_, ...), custom_call_target="tpu_custom_call" | custom-call | tf_op jit(solution)/shard_map/store/pallas_call | solution.py:697

commit v4 on v3

--- a/solution.py
+++ b/solution.py
@@ -582,7 +582,7 @@
     step_part(0, s0)
     s0.core()
     carries[1].wait()
-    sweep(1, {(0, 1): [back_sums[0].gather, s0.scatter]})
+    sweep(1, {(1, 0): [back_sums[0].gather, s0.scatter]})
     back_sums[1].scatter()
     step_part(1, s1)
     s1.core()

time: 96 us -> 95.4 us (level)
  no operation moved by 1% of the time
where the time goes in v4:
time: 95.4 us; the launch traced here: 95.3 us
  Pallas kernels  94.7 us (99%)
    pallas_call x1, Pallas kernels, on_device(): pl.pallas_call(block_kernel, out_shape=shapes, in_specs=[hbm] * 10, out_s...  93.2 us

profile of v4, /device:TPU:1, one launch (start us, length us, event | category | flops | bytes accessed | tf_op | source)
XLA Modules:
  0.0 95.3 jit_solution(4047322248889390557)
XLA Ops:
  0.6 93.2 %block.1 = (f32[128,768]{1,0:T(8,128)S(1)}, f32[128,768]{1,0:T(8,128)S(1)}, f32[128,768]{1,0:T(8,128)S(1)}, f32[2,768,128]{2,1,0:T(8,128)S(1)}, f32[2,96,768]{2,1,0:T(8,128)S(1)}) custom-call(f32[128,768]{1,0:T(8,128)} %tok_h.1, f32[128,768]{1,0:T(8,128)} %gate_h.1, f32[128,768]{1,0:T(8,128)} %cot_h.1, f32[2,4,768]{2,1,0:T(4,128)} %cw_h.1, f32[2,768]{1,0:T(2,128)} %cb_h.1, ...), custom_call_target="tpu_custom_call" | custom-call | tf_op jit(solution)/shard_map/block/pallas_call | solution.py:670
  93.8 1.5 %store.1 = (f32[128,768]{1,0:T(8,128)}, f32[128,768]{1,0:T(8,128)}, f32[128,768]{1,0:T(8,128)}, f32[2,768,128]{2,1,0:T(8,128)}, f32[2,96,768]{2,1,0:T(8,128)}) custom-call(f32[128,768]{1,0:T(8,128)S(1)} %get-tuple-element.10.refs_0_, f32[128,768]{1,0:T(8,128)S(1)} %get-tuple-element.11.refs_1_, f32[128,768]{1,0:T(8,128)S(1)} %get-tuple-element.12.refs_2_, ...), custom_call_target="tpu_custom_call" | custom-call | tf_op jit(solution)/shard_map/store/pallas_call | solution.py:697
